TPU v7x, 512 devices: a whole 4x8x8 slice. The times are simulated.
512 devices in a mesh: row: 16 (over y, core), col: 32 (over x, z).
Axes of the slice: x: 4, y: 8, z: 8, core: 2. Of those that a mesh axis runs over, the one named last changes fastest.
Arguments:
- inverse_block: bfloat16 [16384, 16384], P('row', 'col'), may hold values from -0.375 to 0.375
- tile_mask: int32 [128, 128], P('row', 'col'), may hold values 0 or 1
- factor: bfloat16 [2, 16384, 256], P(None, 'row'), may hold values from -0.29882812 to 0.29882812
- panel_mask: int32 [2, 128], P(None, 'row'), may hold values 0 or 1
- child_top: bfloat16 [256, 256], replicated, may hold values from -0.375 to 0.375
- pivots: float32 [2, 256, 256], replicated, may hold values from -6 to 6
Outputs:
- parent_column: float32 [16384, 256], P(('row', 'col'))
- parent_diag: float32 [256, 256], replicated
- child_upper: float32 [256, 256], replicated
- child_column: float32 [16384, 256], P(('row', 'col'))
- child_diag: float32 [256, 256], replicated
All inputs are finite; a program needn't handle non-finite values. No bound on the sum of `tile_mask` or of `panel_mask` on one device may be relied on, other than what follows from the above.
Results may differ from a plain program's by a relative error of at most 0.0003.
Values may be sent and summed in bfloat16 or wider, within the bound.
No kernel may reach another device: no remote copies, remote signals or barrier semaphores. Data moves between devices by JAX's collectives and lax.ppermute only.
A program may use at most 64 MiB of HBM per device.

v0:
```python
import jax
import jax.numpy as jnp
from jax import lax
from jax.sharding import PartitionSpec as P


def broadcast(value, axis, source):
    kept = jnp.where(lax.axis_index(axis) == source, value, 0).astype(value.dtype)
    return lax.psum(kept, axis)


def shards(inverse_block, tile_mask, factor, panel_mask, child_top, pivots):
    tile_rows, tile_cols = inverse_block.shape
    panel_width = factor.shape[2]
    ncols = lax.axis_size("col")
    ratio = ncols // lax.axis_size("row")
    col_index = lax.axis_index("col")
    root_row = col_index // ratio
    half_index = col_index % ratio
    keep_rows = tile_rows // ncols
    highest = lax.Precision.HIGHEST
    top_float = child_top.astype(jnp.float32)
    mask_factor = tile_mask.astype(jnp.bfloat16)[:, None, :, None]
    masked = (
        inverse_block.reshape(tile_rows // 128, 128, tile_cols // 128, 128) * mask_factor
    ).reshape(tile_rows, tile_cols)
    keep_panel = panel_mask.astype(jnp.bfloat16)
    panels = (
        factor.reshape(2, tile_rows // 128, 128, panel_width) * keep_panel[:, :, None, None]
    ).reshape(2, tile_rows, panel_width)
    arrived = broadcast(panels, "row", root_row)
    received = lax.dynamic_slice_in_dim(arrived, half_index * tile_cols, tile_cols, 1)
    slab = masked
    parent_sum = lax.psum_scatter(
        jnp.dot(slab, received[0], preferred_element_type=jnp.float32),
        "col",
        scatter_dimension=0,
        tiled=True,
    )
    slab = masked
    child_sum = lax.psum_scatter(
        jnp.dot(slab, received[1], preferred_element_type=jnp.float32),
        "col",
        scatter_dimension=0,
        tiled=True,
    )
    parent_column = -parent_sum
    child_column = -(jnp.dot(parent_column, top_float, precision=highest) + child_sum)
    own_rows = lax.dynamic_slice_in_dim(panels, col_index * keep_rows, keep_rows, 1).astype(
        jnp.float32
    )
    pivot_term = jnp.dot(own_rows[0].T, parent_column, precision=highest)
    upper_term = jnp.dot(parent_column.T, own_rows[1], precision=highest)
    pivot_sum, upper_sum = lax.psum((pivot_term, upper_term), ("row", "col"))
    parent_diag = pivots[0] - pivot_sum
    child_upper = -(jnp.dot(parent_diag, top_float, precision=highest) + upper_sum)
    child_pivot_term = jnp.dot(own_rows[1].T, child_column, precision=highest)
    child_sum_total = lax.psum(child_pivot_term, ("row", "col"))
    child_diag = pivots[1] - jnp.dot(top_float.T, child_upper, precision=highest) - child_sum_total
    return (parent_column, parent_diag, child_upper, child_column, child_diag)


def solution(mesh):
    in_specs = (P("row", "col"), P("row", "col"), P(None, "row", None), P(None, "row"), P(), P())
    out_specs = (P(("row", "col"), None), P(), P(), P(("row", "col"), None), P())
    return jax.shard_map(shards, mesh=mesh, in_specs=in_specs, out_specs=out_specs, check_vma=False)
```

profile of v0, /device:TPU:1, one launch (start us, length us, event | category | flops | bytes accessed | tf_op | source)
XLA Modules:
  0.0 876.0 jit_solution(778572854304273017)
XLA Ops:
  7.2 0.0 all-reduce.4.cloned.1.call-start
  7.2 0.7 copy-done.10
  7.9 0.1 broadcast_bitcast_fusion
  8.0 2.6 broadcast_select_fusion
  10.6 0.0 all-reduce.4.cloned.1.call-update
  10.6 0.0 reduce-scatter.3.cloned.1.call-start
  10.7 0.7 copy-done.9
  11.4 0.1 copy.11
  11.5 122.0 %all-reduce.4.cloned.1.call-done = bf16[2,1024,256]{2,1,0:T(8,128)(2,1)} async-done(((bf16[2,1024,256]{2,1,0:T(8,128)(2,1)}), bf16[2,1024,256]{2,1,0:T(8,128)(2,1)}) %all-reduce.4.cloned.1.call-update) | async-done | bytes 1048592 | tf_op jit(solution)/shard_map/psum | solution.py:9
  133.5 0.3 mul.30
  133.9 2.4 fusion.5
  136.3 0.0 reduce-scatter.3.cloned.1.call-update
  136.3 0.0 reduce-scatter.5.cloned.1.call-start
  136.3 2.4 fusion.4
  138.7 0.0 all-reduce.6.cloned.1.call-start
  138.8 217.8 %reduce-scatter.3.cloned.1.call-done = f32[32,256]{1,0:T(8,128)} async-done(((f32[1024,256]{1,0:T(8,128)}), f32[32,256]{1,0:T(8,128)}) %reduce-scatter.3.cloned.1.call-update) | async-done | bytes 32784 | tf_op jit(solution)/shard_map/reduce_scatter | solution.py:34
  356.6 0.8 neg.9
  357.4 1.0 fusion.8
  358.4 1.0 fusion.6
  359.4 222.4 %reduce-scatter.5.cloned.1.call-done = f32[32,256]{1,0:T(8,128)} async-done(((f32[1024,256]{1,0:T(8,128)}), f32[32,256]{1,0:T(8,128)}) %reduce-scatter.5.cloned.1.call-update) | async-done | bytes 32784 | tf_op jit(solution)/shard_map/reduce_scatter | solution.py:41
  581.8 1.0 fusion.3
  582.8 1.0 fusion.7
  583.9 0.0 all-reduce.6.cloned.1.call-update
  583.9 0.9 slice-done
  584.8 0.1 copy.16
  585.0 281.1 %all-reduce.6.cloned.1.call-done = (f32[256,256]{1,0:T(8,128)}, f32[256,256]{1,0:T(8,128)}, f32[256,256]{0,1:T(8,128)}) async-done(((f32[256,256]{1,0:T(8,128)}, f32[256,256]{1,0:T(8,128)}, f32[256,256]{0,1:T(8,128)}), (f32[256,256]{1,0:T(8,128)}, f32[256,256]{1,0:T(8,128)}, f32[256,256]{0,1:T(8,128)})) %all-reduce.6.cloned.1.call-update) | async-done | bytes 786448 | tf_op jit(solution)/shard_map/psum | solution.py:54
  866.1 1.0 bitcast_subtract_fusion
  867.2 0.3 fusion.2
  867.5 0.4 copy-done.2
  867.9 0.4 copy-done.7
  868.2 0.4 fusion.1
  868.6 0.8 copy.14
  (23 shorter events, 0.1 us)
Async XLA Ops:
  7.2 574.7 %copy-start = (bf16[256,256]{1,0:T(8,128)(2,1)S(1)}, bf16[256,256]{1,0:T(8,128)(2,1)}, u32[]{:S(2)}) copy-start(bf16[256,256]{1,0:T(8,128)(2,1)} %param.10) | copy-start | bytes 393220
  7.2 126.3 %all-reduce.4.cloned.1.call-start = ((), (), s32[]{:S(2)}) async-start(), calls=%async_computation.2 | async-start | bytes 2097152 | tf_op jit(solution)/shard_map/psum | solution.py:9
  7.2 0.7 copy-start.10
  10.6 123.3 %copy-start.1 = (bf16[1024,512]{1,0:T(8,128)(2,1)S(1)}, bf16[1024,512]{1,0:T(8,128)(2,1)}, u32[]{:S(2)}) copy-start(bf16[1024,512]{1,0:T(8,128)(2,1)} %param.6) | copy-start | bytes 3145732
  10.6 346.0 %reduce-scatter.3.cloned.1.call-start = ((), (), s32[]{:S(2)}) async-start(), calls=%async_computation.3 | async-start | bytes 1081344 | tf_op jit(solution)/shard_map/reduce_scatter | solution.py:34
  10.6 0.8 copy-start.9
  136.3 445.5 %reduce-scatter.5.cloned.1.call-start = ((), (), s32[]{:S(2)}) async-start(), calls=%async_computation.4 | async-start | bytes 1081344 | tf_op jit(solution)/shard_map/reduce_scatter | solution.py:41
  138.7 727.4 %all-reduce.6.cloned.1.call-start = ((), (), s32[]{:S(2)}) async-start(), calls=%async_computation.5 | async-start | bytes 1572864 | tf_op jit(solution)/shard_map/psum | solution.py:54
  357.4 224.5 %copy-start.5 = (f32[32,256]{1,0:T(8,128)}, f32[32,256]{1,0:T(8,128)S(1)}, u32[]{:S(2)}) copy-start(f32[32,256]{1,0:T(8,128)S(1)} %neg.9) | copy-start | bytes 98308
  582.8 1.0 copy-start.8
  583.9 1.0 slice-start
  583.9 282.2 %copy-start.4 = (f32[2,256,256]{2,1,0:T(8,128)S(1)}, f32[2,256,256]{2,1,0:T(8,128)}, u32[]{:S(2)}) copy-start(f32[2,256,256]{2,1,0:T(8,128)} %param.11) | copy-start | bytes 1572868
  866.1 1.0 copy-start.6
  867.1 0.7 copy-start.2
  867.2 1.0 copy-start.7
  867.9 0.8 copy-start.3
Sparse Core Ops, SparseCore 0:
  10.7 122.7 all-reduce.3
  137.9 218.6 reduce-scatter.2
  361.0 220.8 reduce-scatter.4
  587.8 278.3 all-reduce.5
where the time goes:
time: 877 us; the launch traced here: 876 us
  waiting for transfers between devices  843 us (96%)
  between operations  13.9 us (2%)
  matrix products  9.43 us (1%)
    psum x1, waiting for transfers between devices, shards(): pivot_sum, upper_sum = lax.psum((pivot_term, upper_term), ('row', 'col'))  281 us
    reduce_scatter x1, waiting for transfers between devices, shards(): lax.psum_scatter(jnp.dot(slab, received[1], preferred_element_type=jnp.fl...  222 us
    reduce_scatter x1, waiting for transfers between devices, shards(): lax.psum_scatter(jnp.dot(slab, received[0], preferred_element_type=jnp.fl...  218 us
    psum x1, waiting for transfers between devices, broadcast(): return lax.psum(kept, axis)  122 us
  transfers between devices with their start and end apart: 4, of which 4 were waited for; matrix products, arithmetic and copies ran while one was open for 1% of the time, Pallas kernels for 0%

commit v1 on v0

v1 whole, which is shorter than its diff:
```python
import jax
import jax.numpy as jnp
from jax import lax
from jax.sharding import Mesh, PartitionSpec as P

ROW = ("y", "core")
COL = ("x", "z")
HIGHEST = lax.Precision.HIGHEST
LIMIT = 32766.0


def mm(a, b, ca, cb):
    return lax.dot_general(
        a, b, (((ca,), (cb,)), ((), ())), precision=HIGHEST, preferred_element_type=jnp.float32
    )


def scale_of(value, axes):
    top = jnp.maximum(jnp.max(jnp.abs(value), axis=axes, keepdims=True), 1e-30)
    power = jnp.ceil(jnp.log2(top))
    mantissa = jnp.ceil(top * jnp.exp2(14.0 - power) + 2.0)
    code = (power.astype(jnp.int32) << 16) | mantissa.astype(jnp.int32)
    return mantissa * jnp.exp2(power - 14.0), code


def scale_from(code):
    return (code & 0xFFFF).astype(jnp.float32) * jnp.exp2((code >> 16).astype(jnp.float32) - 14.0)


def join(high, low):
    return (high << 16) | (low & 0xFFFF)


def part(joined):
    return joined >> 16, (joined << 16) >> 16


def exchange(partial, axis):
    rows = partial.shape[3]
    step, code = scale_of(partial, (3,))
    whole = jnp.round(partial * (LIMIT / step)).astype(jnp.int32)
    body = join(whole[0], whole[1])
    lane = lax.broadcasted_iota(jnp.int32, body.shape[:2] + (128,), 2)
    code = jnp.where(lane < 64, code[0], code[1])
    got = lax.all_to_all(jnp.concatenate([body, code], axis=2), axis, 0, 0, tiled=True)
    step = scale_from(jnp.stack([got[:, :, rows], got[:, :, rows + 64]])) * (1.0 / LIMIT)
    whole = jnp.stack(part(got[:, :, :rows])).astype(jnp.float32)
    return jnp.sum(whole * step[..., None], axis=1)


def shards(inverse_block, tile_mask, factor, panel_mask, child_top, pivots):
    rows, cols = inverse_block.shape
    width = factor.shape[2]
    ny, ncore = lax.axis_size("y"), lax.axis_size("core")
    nrow = ny * ncore
    nx, nz = lax.axis_size("x"), lax.axis_size("z")
    ncol = nx * nz
    core = lax.axis_index("core")
    col = lax.axis_index(COL)
    halves = rows // cols
    piece = cols // nrow
    own_rows = rows // ncol
    slot = width // ncol

    pairs = []
    for s in range(nrow):
        for q in range(ncol):
            r, h = q // halves, q % halves
            pairs.append((s * ncol + q, r * ncol + halves * s + h))
    to_row, half = col // halves, col % halves
    start = half * cols + (to_row % ncore) * (cols // ncore) + (to_row // ncore) * piece
    sent = lax.dynamic_slice_in_dim(factor, start, piece, 1)
    kept = lax.dynamic_slice_in_dim(panel_mask, start // 128, 1, 1)[:, :, None]
    sent = jnp.where(kept == 1, sent, 0).astype(jnp.bfloat16)
    sent = jnp.concatenate([sent[0], sent[1]], axis=1)
    mine = lax.ppermute(sent, ROW + COL, pairs)
    same = lax.all_to_all(
        jnp.broadcast_to(mine[None], (ny,) + mine.shape), "y", 0, 0, tiled=True
    ).reshape(cols // ncore, 2 * width)
    other = lax.ppermute(same, "core", [(0, 1), (1, 0)])
    first = jnp.where(core == 0, same, other)
    second = jnp.where(core == 0, other, same)
    panel = jnp.concatenate([first, second], axis=0)

    keep = panel_mask.astype(jnp.bfloat16)
    panels = (
        factor.reshape(2, rows // 128, 128, width) * keep[:, :, None, None]
    ).reshape(2, rows, width)
    joined = jnp.concatenate([panels[0], panels[1]], axis=1).astype(jnp.float32)

    mask = tile_mask.astype(jnp.bfloat16)[:, None, :, None]
    masked = (inverse_block.reshape(rows // 128, 128, cols // 128, 128) * mask).reshape(rows, cols)
    partial = lax.dot_general(
        panel, masked, (((0,), (1,)), ((), ())), preferred_element_type=jnp.float32
    )
    total = exchange(partial.reshape(2, nx, nz * slot, rows), "x")
    total = exchange(total.reshape(2, nz, slot, rows), "z")

    gram_parent = mm(total[0], joined, 1, 0)
    gram_child = mm(total[1], joined[:, width:], 1, 0)
    gram = jnp.concatenate([gram_parent[:, :width], gram_parent[:, width:], gram_child], axis=0)
    gram = gram + lax.ppermute(gram, "core", [(0, 1), (1, 0)])
    spread = lax.all_to_all(jnp.broadcast_to(gram[None], (ny,) + gram.shape), "y", 0, 0, tiled=True)
    gram = jnp.sum(spread.reshape((ny, 3, slot, width)), axis=0)

    step, code = scale_of(gram, (1, 2))
    whole = jnp.round(gram * (LIMIT / step)).astype(jnp.int32)
    packed = join(whole[:, :, : width // 2], whole[:, :, width // 2 :]).reshape(3 * slot, width // 2)
    row_step, row_code = scale_of(total, (0, 1, 2))
    fixed = jnp.round(total * (float(1 << 30) / row_step)).astype(jnp.int32)
    fixed = fixed.reshape(2, slot // 2, 2, nx, nz, own_rows).transpose(3, 4, 1, 2, 0, 5)
    fixed = fixed.reshape(ncol, slot // 2, 128)
    codes = jnp.broadcast_to(
        jnp.concatenate([code.reshape(3, 1), row_code.reshape(1, 1)]), (4, 128)
    )
    same_for_all = jnp.concatenate([packed, codes], axis=0)
    same_for_all = jnp.broadcast_to(same_for_all[None], (ncol,) + same_for_all.shape)
    last = lax.all_to_all(jnp.concatenate([same_for_all, fixed], axis=1), COL, 0, 0, tiled=True)
    scales = scale_from(last[:, 3 * slot : 3 * slot + 4, :])
    high, low = part(last[:, : 3 * slot].reshape(ncol, 3, slot, width // 2))
    unit = scales[:, :3, :1, None] * (1.0 / LIMIT)
    grams = jnp.concatenate([high.astype(jnp.float32) * unit, low.astype(jnp.float32) * unit], axis=3)
    grams = grams.transpose(1, 0, 2, 3).reshape(3, width, width)
    sums = last[:, 3 * slot + 4 :].astype(jnp.float32) * (scales[:, 3:4, :1] * (1.0 / (1 << 30)))
    sums = sums.reshape(ncol, slot // 2, 2, 2, own_rows).transpose(3, 4, 0, 1, 2).reshape(2, own_rows, width)

    top = child_top.astype(jnp.float32)
    parent_column = -sums[0]
    child_column = -(mm(parent_column, top, 1, 0) + sums[1])
    parent_diag = pivots[0] + grams[0].T
    child_upper = mm(-parent_diag, top, 1, 0) + grams[1]
    child_diag = pivots[1] - mm(top, child_upper, 0, 0) - mm(grams[1], top, 0, 0) + grams[2].T
    return (parent_column, parent_diag, child_upper, child_column, child_diag)


def solution(mesh):
    grid = Mesh(mesh.devices.reshape(8, 2, 4, 8), ROW + COL)
    in_specs = (P(ROW, COL), P(ROW, COL), P(None, ROW, None), P(None, ROW), P(), P())
    out_specs = (P(ROW + COL, None), P(), P(), P(ROW + COL, None), P())
    return jax.shard_map(shards, mesh=grid, in_specs=in_specs, out_specs=out_specs, check_vma=False)
```

time: 877 us -> 138 us (0.16)
  waiting for transfers between devices: 843 us -> 52.3 us
  starting transfers between devices: 0.16 us -> 39.3 us
  blocking collectives: 0 us -> 22.5 us
  between operations: 13.9 us -> 2.05 us
    reduce_scatter x2 -> x0, waiting for transfers between devices: 440 us -> none  [the longest x1 222 us: shards(): lax.psum_scatter(jnp.dot(slab, received[1], preferred_element_type=jnp.fl...]
    psum x2 -> x0, waiting for transfers between devices: 403 us -> none  [the longest x1 281 us: shards(): pivot_sum, upper_sum = lax.psum((pivot_term, upper_term), ('row', 'col'))]
    all_to_all x0 -> x4, waiting for transfers between devices: none -> 49.5 us  [the longest x2 27 us: exchange(): lax.all_to_all(jnp.concatenate([body, code], axis=2), axis, 0, 0, tiled=T...]
    all_to_all x0 -> x1, blocking collectives: none -> 22.5 us  [shards(): lax.all_to_all(jnp.broadcast_to(mine[None], (ny,) + mine.shape), 'y', 0,...]
    all_to_all x0 -> x4, starting transfers between devices: none -> 20 us  [the longest x2 12.7 us: exchange(): lax.all_to_all(jnp.concatenate([body, code], axis=2), axis, 0, 0, tiled=T...]
    ppermute x0 -> x3, starting transfers between devices: none -> 19.3 us  [the longest x1 7.53 us: shards(): other = lax.ppermute(same, 'core', [(0, 1), (1, 0)])]
  transfers between devices with their start and end apart: 4 -> 7, of which waited for: 4 -> 7; matrix products, arithmetic and copies ran while one was open for 1% -> 2% of each run, Pallas kernels for 0% -> 0%
where the time goes in v1:
time: 138 us; the launch traced here: 135 us
  waiting for transfers between devices  52.3 us (38%)
  starting transfers between devices  39.3 us (28%)
  blocking collectives  22.5 us (16%)
  other arithmetic  8.64 us (6%)
  local copies, waits for them, and re-layouts  6.92 us (5%)
  matrix products  3.66 us (3%)
  between operations  2.05 us (1%)
    all_to_all x2, waiting for transfers between devices, exchange(): lax.all_to_all(jnp.concatenate([body, code], axis=2), axis, 0, 0, tiled=T...  27 us
    all_to_all x1, blocking collectives, shards(): lax.all_to_all(jnp.broadcast_to(mine[None], (ny,) + mine.shape), 'y', 0,...  22.5 us
    all_to_all x1, waiting for transfers between devices, shards(): lax.all_to_all(jnp.concatenate([same_for_all, fixed], axis=1), COL, 0, 0,...  14.2 us
    all_to_all x2, starting transfers between devices, exchange(): lax.all_to_all(jnp.concatenate([body, code], axis=2), axis, 0, 0, tiled=T...  12.7 us
    all_to_all x1, waiting for transfers between devices, shards(): lax.all_to_all(jnp.broadcast_to(gram[None], (ny,) + gram.shape), 'y', 0,...  8.36 us
    ppermute x1, starting transfers between devices, shards(): other = lax.ppermute(same, 'core', [(0, 1), (1, 0)])  7.53 us
    ppermute x1, starting transfers between devices, shards(): mine = lax.ppermute(sent, ROW + COL, pairs)  7.19 us
    ppermute x1, starting transfers between devices, shards(): gram = gram + lax.ppermute(gram, 'core', [(0, 1), (1, 0)])  4.62 us
  transfers between devices with their start and end apart: 7, of which 7 were waited for; matrix products, arithmetic and copies ran while one was open for 2% of the time, Pallas kernels for 0%

profile of v1, /device:TPU:1, one launch (start us, length us, event | category | flops | bytes accessed | tf_op | source)
XLA Modules:
  0.0 135.3 jit_solution(3642892140799333464)
XLA Ops:
  0.7 0.9 compare_reduce_fusion
  1.6 0.8 dynamic-slice_select_fusion
  2.4 7.2 %collective-permute-start = (bf16[32,512]{1,0:T(8,128)(2,1)S(1)}, bf16[32,512]{1,0:T(8,128)(2,1)S(1)}, u32[]{:S(2)}, u32[]{:S(2)}) collective-permute-start(bf16[32,512]{1,0:T(8,128)(2,1)S(1)} %pad_maximum_fusion), channel_id=1, source_target_pairs={{0,0},{1,1},{2,32},{3,33},{4,64},{5,65},{6,96},{7,97},{8,128},{9,1... | collective-permute-start | bytes 98312 | tf_op jit(solution)/shard_map/ppermute | solution.py:76
  9.6 1.6 %collective-permute-done = bf16[32,512]{1,0:T(8,128)(2,1)S(1)} collective-permute-done((bf16[32,512]{1,0:T(8,128)(2,1)S(1)}, bf16[32,512]{1,0:T(8,128)(2,1)S(1)}, u32[]{:S(2)}, u32[]{:S(2)}) %collective-permute-start) | collective-permute-done | bytes 32800 | tf_op jit(solution)/shard_map/ppermute | solution.py:76
  11.3 22.5 %all_to_all.25 = bf16[8,32,512]{2,1,0:T(8,128)(2,1)S(1)} all-to-all(bf16[8,32,512]{2,1,0:T(8,128)(2,1)S(1)} %broadcast_in_dim.89), channel_id=1, replica_groups=mesh['y'=8,'core'=2,'x'=4,'z'=8] {'y'}, dimensions={0} | all-to-all | bytes 524288 | tf_op jit(solution)/shard_map/all_to_all | solution.py:77
  33.7 7.5 %collective-permute-start.1 = (bf16[256,512]{1,0:T(8,128)(2,1)S(1)}, bf16[256,512]{1,0:T(8,128)(2,1)S(1)}, u32[]{:S(2)}, u32[]{:S(2)}) collective-permute-start(bf16[256,512]{1,0:T(8,128)(2,1)S(1)} %bitcast.166), channel_id=1, source_target_pairs={{0,32},{32,0},{1,33},{33,1},{2,34},{34,2},{3,35},{35,3},{4,36},{36... | collective-permute-start | bytes 786440 | tf_op jit(solution)/shard_map/ppermute | solution.py:80
  41.3 0.7 convert_element_type.155
  42.0 0.3 collective-permute-done.1
  43.3 0.9 abs_reduce_fusion
  44.8 1.1 pad_add_fusion
  45.9 3.5 %all-to-all-start.1 = ((s32[4,64,1152]{2,1,0:T(8,128)}), s32[4,64,1152]{2,1,0:T(8,128)S(1)}, u32[]{:S(2)}, u32[]{:S(2)}) async-start(s32[4,64,1152]{2,1,0:T(8,128)} %pad_add_fusion), calls=%async_computation.1 | async-start | bytes 2359296 | tf_op jit(solution)/shard_map/all_to_all | solution.py:45
  49.4 16.4 %all-to-all-done.1 = s32[4,64,1152]{2,1,0:T(8,128)S(1)} async-done(((s32[4,64,1152]{2,1,0:T(8,128)}), s32[4,64,1152]{2,1,0:T(8,128)S(1)}, u32[]{:S(2)}, u32[]{:S(2)}) %all-to-all-start.1) | async-done | bytes 1179680 | tf_op jit(solution)/shard_map/all_to_all | solution.py:45
  67.3 0.7 pad_add_fusion.2
  68.0 9.2 %all-to-all-start.2 = ((s32[8,8,1152]{2,1,0:T(8,128)}), s32[8,8,1152]{2,1,0:T(8,128)S(1)}, u32[]{:S(2)}, u32[]{:S(2)}) async-start(s32[8,8,1152]{2,1,0:T(8,128)} %pad_add_fusion.2), calls=%async_computation.2 | async-start | bytes 589824 | tf_op jit(solution)/shard_map/all_to_all | solution.py:45
  77.4 10.6 %all-to-all-done.2 = s32[8,8,1152]{2,1,0:T(8,128)S(1)} async-done(((s32[8,8,1152]{2,1,0:T(8,128)}), s32[8,8,1152]{2,1,0:T(8,128)S(1)}, u32[]{:S(2)}, u32[]{:S(2)}) %all-to-all-start.2) | async-done | bytes 294944 | tf_op jit(solution)/shard_map/all_to_all | solution.py:45
  88.0 0.4 slice_reduce_fusion.3
  88.9 0.5 fusion.11
  89.4 4.6 %collective-permute-start.2 = (f32[24,256]{1,0:T(8,128)S(1)}, f32[24,256]{1,0:T(8,128)S(1)}, u32[]{:S(2)}, u32[]{:S(2)}) collective-permute-start(f32[24,256]{1,0:T(8,128)S(1)} %pad_maximum_fusion.1), channel_id=1, source_target_pairs={{0,32},{32,0},{1,33},{33,1},{2,34},{34,2},{3,35},{35,3},{4,36},{36... | collective-permute-start | bytes 73736 | tf_op jit(solution)/shard_map/ppermute | solution.py:102
  94.1 0.8 collective-permute-done.2
  94.9 0.7 broadcast_in_dim.98
  95.6 3.4 %all-to-all-start.3 = ((f32[8,24,256]{2,1,0:T(8,128)}), f32[8,24,256]{2,1,0:T(8,128)S(1)}, u32[]{:S(2)}, u32[]{:S(2)}) async-start(f32[8,24,256]{2,1,0:T(8,128)} %broadcast_in_dim.98), calls=%async_computation.3 | async-start | bytes 393216 | tf_op jit(solution)/shard_map/all_to_all | solution.py:103
  99.0 0.6 abs_reduce_fusion.2
  101.0 8.4 %all-to-all-done.3 = f32[8,24,256]{2,1,0:T(8,128)S(1)} async-done(((f32[8,24,256]{2,1,0:T(8,128)}), f32[8,24,256]{2,1,0:T(8,128)S(1)}, u32[]{:S(2)}, u32[]{:S(2)}) %all-to-all-start.3) | async-done | bytes 196640 | tf_op jit(solution)/shard_map/all_to_all | solution.py:103
  110.2 0.9 pad_add_fusion.1
  111.0 3.9 %all-to-all-start.4 = ((s32[32,32,128]{2,1,0:T(8,128)}), s32[32,32,128]{2,1,0:T(8,128)S(1)}, u32[]{:S(2)}, u32[]{:S(2)}) async-start(s32[32,32,128]{2,1,0:T(8,128)} %pad_add_fusion.1), calls=%async_computation.4 | async-start | bytes 1048576 | tf_op jit(solution)/shard_map/all_to_all | solution.py:118
  115.2 14.2 %all-to-all-done.4 = s32[32,32,128]{2,1,0:T(8,128)S(1)} async-done(((s32[32,32,128]{2,1,0:T(8,128)}), s32[32,32,128]{2,1,0:T(8,128)S(1)}, u32[]{:S(2)}, u32[]{:S(2)}) %all-to-all-start.4) | async-done | bytes 524320 | tf_op jit(solution)/shard_map/all_to_all | solution.py:118
  130.1 0.8 copy.130
  130.9 0.4 convolution_add_fusion
  131.3 0.4 fusion.3
  132.0 0.8 copy.131
  133.7 0.7 copy.129
  134.4 0.9 fusion.4
  (87 shorter events, 7.1 us)
Async XLA Ops:
  0.6 130.3 %copy-start = (bf16[256,256]{1,0:T(8,128)(2,1)S(1)}, bf16[256,256]{1,0:T(8,128)(2,1)}, u32[]{:S(2)}) copy-start(bf16[256,256]{1,0:T(8,128)(2,1)} %param.10) | copy-start | bytes 393220
  2.4 8.8 %collective-permute-start = (bf16[32,512]{1,0:T(8,128)(2,1)S(1)}, bf16[32,512]{1,0:T(8,128)(2,1)S(1)}, u32[]{:S(2)}, u32[]{:S(2)}) collective-permute-start(bf16[32,512]{1,0:T(8,128)(2,1)S(1)} %pad_maximum_fusion), channel_id=1, source_target_pairs={{0,0},{1,1},{2,32},{3,33},{4,64},{5,65},{6,96},{7,97},{8,128},{9,1... | collective-permute-start | bytes 98312 | tf_op jit(solution)/shard_map/ppermute | solution.py:76
  33.7 8.7 %collective-permute-start.1 = (bf16[256,512]{1,0:T(8,128)(2,1)S(1)}, bf16[256,512]{1,0:T(8,128)(2,1)S(1)}, u32[]{:S(2)}, u32[]{:S(2)}) collective-permute-start(bf16[256,512]{1,0:T(8,128)(2,1)S(1)} %bitcast.166), channel_id=1, source_target_pairs={{0,32},{32,0},{1,33},{33,1},{2,34},{34,2},{3,35},{35,3},{4,36},{36... | collective-permute-start | bytes 786440 | tf_op jit(solution)/shard_map/ppermute | solution.py:80
  42.0 1.2 copy-start.5
  44.8 4.7 %copy-start.4 = (s32[2,8]{1,0:T(2,128)S(1)}, s32[2,8]{1,0:T(2,128)}, u32[]{:S(2)}) copy-start(s32[2,8]{1,0:T(2,128)} %param.9) | copy-start | bytes 196
  45.9 19.9 %all-to-all-start.1 = ((s32[4,64,1152]{2,1,0:T(8,128)}), s32[4,64,1152]{2,1,0:T(8,128)S(1)}, u32[]{:S(2)}, u32[]{:S(2)}) async-start(s32[4,64,1152]{2,1,0:T(8,128)} %pad_add_fusion), calls=%async_computation.1 | async-start | bytes 2359296 | tf_op jit(solution)/shard_map/all_to_all | solution.py:45
  66.7 10.5 %copy-start.1 = (bf16[2,1024,256]{2,1,0:T(8,128)(2,1)S(1)}, bf16[2,1024,256]{2,1,0:T(8,128)(2,1)}, u32[]{:S(2)}) copy-start(bf16[2,1024,256]{2,1,0:T(8,128)(2,1)} %param.8) | copy-start | bytes 3145732
  68.0 20.0 %all-to-all-start.2 = ((s32[8,8,1152]{2,1,0:T(8,128)}), s32[8,8,1152]{2,1,0:T(8,128)S(1)}, u32[]{:S(2)}, u32[]{:S(2)}) async-start(s32[8,8,1152]{2,1,0:T(8,128)} %pad_add_fusion.2), calls=%async_computation.2 | async-start | bytes 589824 | tf_op jit(solution)/shard_map/all_to_all | solution.py:45
  89.4 5.5 %collective-permute-start.2 = (f32[24,256]{1,0:T(8,128)S(1)}, f32[24,256]{1,0:T(8,128)S(1)}, u32[]{:S(2)}, u32[]{:S(2)}) collective-permute-start(f32[24,256]{1,0:T(8,128)S(1)} %pad_maximum_fusion.1), channel_id=1, source_target_pairs={{0,32},{32,0},{1,33},{33,1},{2,34},{34,2},{3,35},{35,3},{4,36},{36... | collective-permute-start | bytes 73736 | tf_op jit(solution)/shard_map/ppermute | solution.py:102
  95.6 13.8 %all-to-all-start.3 = ((f32[8,24,256]{2,1,0:T(8,128)}), f32[8,24,256]{2,1,0:T(8,128)S(1)}, u32[]{:S(2)}, u32[]{:S(2)}) async-start(f32[8,24,256]{2,1,0:T(8,128)} %broadcast_in_dim.98), calls=%async_computation.3 | async-start | bytes 393216 | tf_op jit(solution)/shard_map/all_to_all | solution.py:103
  100.4 14.5 %copy-start.3 = (f32[2,256,256]{2,1,0:T(8,128)S(1)}, f32[2,256,256]{2,1,0:T(8,128)}, u32[]{:S(2)}) copy-start(f32[2,256,256]{2,1,0:T(8,128)} %param.11) | copy-start | bytes 1572868
  111.0 18.4 %all-to-all-start.4 = ((s32[32,32,128]{2,1,0:T(8,128)}), s32[32,32,128]{2,1,0:T(8,128)S(1)}, u32[]{:S(2)}, u32[]{:S(2)}) async-start(s32[32,32,128]{2,1,0:T(8,128)} %pad_add_fusion.1), calls=%async_computation.4 | async-start | bytes 1048576 | tf_op jit(solution)/shard_map/all_to_all | solution.py:118
  131.3 2.3 %copy-start.2 = (f32[256,256]{1,0:T(8,128)}, f32[256,256]{1,0:T(8,128)S(1)}, u32[]{:S(2)}) copy-start(f32[256,256]{1,0:T(8,128)S(1)} %convolution_add_fusion) | copy-start | bytes 786436

commit v2 on v1

v2 whole, which is shorter than its diff:
```python
import jax
import jax.numpy as jnp
from jax import lax
from jax.experimental import pallas as pl
from jax.experimental.pallas import tpu as pltpu
from jax.sharding import Mesh, PartitionSpec as P

ROW = ("y", "core")
COL = ("x", "z")
LIMIT = 32766.0
FIXED = float(1 << 30)
VMEM = pl.BlockSpec(memory_space=pltpu.VMEM)
SMEM = pl.BlockSpec(memory_space=pltpu.SMEM)


def scale_of(top):
    top = jnp.maximum(top, 1e-30)
    power = jnp.ceil(jnp.log2(top))
    mantissa = jnp.ceil(top * jnp.exp2(14.0 - power) + 2.0)
    code = (power.astype(jnp.int32) << 16) | mantissa.astype(jnp.int32)
    return mantissa * jnp.exp2(power - 14.0), code


def scale_from(code):
    return (code & 0xFFFF).astype(jnp.float32) * jnp.exp2((code >> 16).astype(jnp.float32) - 14.0)


def whole(value, factor):
    return jnp.round(value * factor).astype(jnp.int32)


def join(high, low):
    return (high << 16) | (low & 0xFFFF)


def part(joined):
    return (joined >> 16).astype(jnp.float32), ((joined << 16) >> 16).astype(jnp.float32)


def split(value):
    high = value.astype(jnp.bfloat16)
    rest = value - high.astype(jnp.float32)
    middle = rest.astype(jnp.bfloat16)
    return high, middle, (rest - middle.astype(jnp.float32)).astype(jnp.bfloat16)


def dot(a, b, ca, cb):
    return lax.dot_general(a, b, (((ca,), (cb,)), ((), ())), preferred_element_type=jnp.float32)


def encode_rows(high, low):
    high_step, high_code = scale_of(jnp.max(jnp.abs(high), axis=1, keepdims=True))
    low_step, low_code = scale_of(jnp.max(jnp.abs(low), axis=1, keepdims=True))
    body = join(whole(high, LIMIT / high_step), whole(low, LIMIT / low_step))
    lane = lax.broadcasted_iota(jnp.int32, (high.shape[0], 128), 1)
    return body, jnp.where(lane < 64, high_code, low_code)


def decode_rows(ref, index, rows):
    high, low = part(ref[index, :, :rows])
    code = ref[index, :, rows:]
    return high * (scale_from(code[:, :1]) * (1.0 / LIMIT)), low * (scale_from(code[:, 64:65]) * (1.0 / LIMIT))


def piece_kernel(at_ref, mask_ref, factor_ref, out_ref):
    width = factor_ref.shape[2]
    block = at_ref[0] * factor_ref.shape[1] // 128
    for k in range(2):
        kept = jnp.where(mask_ref[k, block] == 1, factor_ref[k], 0.0)
        out_ref[:, k * width : k * width + width] = kept.astype(jnp.bfloat16)


def product_kernel(mask_ref, core_ref, same_ref, other_ref, inverse_ref, out_ref, turned, product):
    width = same_ref.shape[1] // 2
    rows, cols = inverse_ref.shape
    first = core_ref[0] == 0
    turned[:, : cols // 2] = jnp.where(first, same_ref[...], other_ref[...]).T
    turned[:, cols // 2 :] = jnp.where(first, other_ref[...], same_ref[...]).T
    step = 256
    for i in range(rows // step):
        blocks = []
        for j in range(cols // 128):
            column = [
                jnp.where(
                    mask_ref[i * step // 128 + h, j] == 1,
                    inverse_ref[i * step + h * 128 : i * step + h * 128 + 128, j * 128 : j * 128 + 128],
                    0.0,
                ).astype(jnp.bfloat16)
                for h in range(step // 128)
            ]
            blocks.append(jnp.concatenate(column, axis=0))
        masked = jnp.concatenate(blocks, axis=1)
        product[:, i * step : i * step + step] = dot(turned[...], masked, 1, 1)
    count = out_ref.shape[1]
    for x in range(out_ref.shape[0]):
        body, code = encode_rows(
            product[x * count : x * count + count, :],
            product[width + x * count : width + x * count + count, :],
        )
        out_ref[x, :, :rows] = body
        out_ref[x, :, rows:] = code


def middle_kernel(in_ref, out_ref):
    rows = in_ref.shape[2] - 128
    high, low = decode_rows(in_ref, 0, rows)
    for i in range(1, in_ref.shape[0]):
        more_high, more_low = decode_rows(in_ref, i, rows)
        high, low = high + more_high, low + more_low
    body, code = encode_rows(high, low)
    out_ref[:, :rows] = body
    out_ref[:, rows:] = code


def encode_grams(grams, store):
    for k, gram in enumerate(grams):
        half = gram.shape[1] // 2
        top = jnp.max(jnp.max(jnp.abs(gram), axis=1, keepdims=True), axis=0, keepdims=True)
        step, code = scale_of(jnp.broadcast_to(top, (1, half)))
        inverse = LIMIT / step
        store(k, join(whole(gram[:, :half], inverse), whole(gram[:, half:], inverse)), code)


def gram_kernel(mask_ref, in_ref, factor_ref, out_ref, total_ref):
    rows = in_ref.shape[2] - 128
    slot = in_ref.shape[1]
    high, low = decode_rows(in_ref, 0, rows)
    for i in range(1, in_ref.shape[0]):
        more_high, more_low = decode_rows(in_ref, i, rows)
        high, low = high + more_high, low + more_low
    total_ref[0], total_ref[1] = high, low
    pieces = jnp.concatenate([p.astype(jnp.float32) for p in split(high) + split(low)], axis=0)
    pieces = pieces.astype(jnp.bfloat16)
    sums = []
    for k in range(2):
        panel = jnp.concatenate(
            [
                jnp.where(mask_ref[k, i] == 1, factor_ref[k, i * 128 : i * 128 + 128, :], 0.0).astype(jnp.bfloat16)
                for i in range(rows // 128)
            ],
            axis=0,
        )
        found = dot(pieces, panel, 1, 0)
        for s in range(2):
            b = 3 * slot * s
            sums.append(
                found[b : b + slot] + found[b + slot : b + 2 * slot] + found[b + 2 * slot : b + 3 * slot]
            )
    half = sums[0].shape[1] // 2

    def store(k, body, code):
        for r in range(out_ref.shape[0]):
            out_ref[r, k * slot : k * slot + slot, :] = body
            out_ref[r, 3 * slot + k : 3 * slot + k + 1, :] = code

    filler = jnp.zeros((out_ref.shape[1] - 3 * slot - 3, half), jnp.int32)
    for r in range(out_ref.shape[0]):
        out_ref[r, 3 * slot + 3 :, :] = filler
    encode_grams((sums[0], sums[2], sums[3]), store)


def decode_gram(ref, index, k, slot):
    high, low = part(ref[index, k * slot : k * slot + slot, :])
    unit = scale_from(ref[index, 3 * slot + k : 3 * slot + k + 1, :]) * (1.0 / LIMIT)
    return jnp.concatenate([high * unit, low * unit], axis=1)


def spread_kernel(in_ref, fixed_ref, code_ref, out_ref):
    slot = (in_ref.shape[1] - 8) // 3
    grams = []
    for k in range(3):
        gram = decode_gram(in_ref, 0, k, slot)
        for i in range(1, in_ref.shape[0]):
            gram = gram + decode_gram(in_ref, i, k, slot)
        grams.append(gram)

    def store(k, body, code):
        for c in range(out_ref.shape[0]):
            out_ref[c, k * slot : k * slot + slot, :] = body
            out_ref[c, 3 * slot + k : 3 * slot + k + 1, :] = code

    encode_grams(grams, store)
    for c in range(out_ref.shape[0]):
        out_ref[c, 3 * slot + 3 : 3 * slot + 4, :] = code_ref[...]
        out_ref[c, 3 * slot + 4 :, :] = fixed_ref[c]


def exact(a, b, ca, cb):
    parts = split(a)
    return dot(parts[0], b, ca, cb) + (dot(parts[1], b, ca, cb) + dot(parts[2], b, ca, cb))


def final_kernel(in_ref, top_ref, pivots_ref, parent_column, parent_diag, child_upper, child_column, child_diag):
    ncol = in_ref.shape[0]
    width = top_ref.shape[0]
    slot = width // ncol
    top = top_ref[...]
    grams = []
    for k in range(3):
        high, low = part(in_ref[:, k * slot : k * slot + slot, :])
        unit = scale_from(in_ref[:, 3 * slot + k : 3 * slot + k + 1, :]) * (1.0 / LIMIT)
        high = (high * unit).reshape(width, width // 2)
        grams.append(jnp.concatenate([high, (low * unit).reshape(width, width // 2)], axis=1))
    diag = pivots_ref[0] + grams[0].T
    parent_diag[...] = diag
    upper = grams[1] - exact(diag, top, 1, 0)
    child_upper[...] = upper
    parts = split(upper)
    turned = dot(top, parts[0], 0, 0) + (dot(top, parts[1], 0, 0) + dot(top, parts[2], 0, 0))
    child_diag[...] = pivots_ref[1] - turned - exact(grams[1], top, 0, 0) + grams[2].T

    unit = scale_from(in_ref[:, 3 * slot + 3 : 3 * slot + 4, :]) * (1.0 / FIXED)
    count = ncol * slot // 2
    sums = (in_ref[:, 3 * slot + 4 :, :].astype(jnp.float32) * unit).reshape(count, 128)
    row = lax.broadcasted_iota(jnp.int32, (count, width), 0)
    column = lax.broadcasted_iota(jnp.int32, (count, width), 1)
    placed = None
    for h in range(2):
        choice = jnp.where(column == 2 * row + h, 1.0, 0.0).astype(jnp.bfloat16)
        for piece in split(sums):
            term = dot(piece, choice, 0, 0)[64 * h : 64 * h + 64]
            placed = term if placed is None else placed + term
    own = placed.shape[0] // 2
    parent_column[...] = -placed[:own]
    child_column[...] = exact(placed[:own], top, 1, 0) - placed[own:]


def call(kernel, out_shape, smem=0, scratch=(), results=pltpu.VMEM, name=None):
    single = isinstance(out_shape, jax.ShapeDtypeStruct)
    shapes = [out_shape] if single else list(out_shape)
    if results is not None:
        shapes = [results(s.shape, s.dtype) for s in shapes]

    def run(*args):
        found = pl.pallas_call(
            kernel,
            out_shape=shapes,
            in_specs=[SMEM] * smem + [VMEM] * (len(args) - smem),
            out_specs=[VMEM] * len(shapes),
            scratch_shapes=list(scratch),
            name=name,
        )(*args[:smem], *(pltpu.with_memory_space_constraint(a, pltpu.VMEM) for a in args[smem:]))
        return found[0] if single else found

    return run


def shards(inverse_block, tile_mask, factor, panel_mask, child_top, pivots):
    rows, cols = inverse_block.shape
    width = factor.shape[2]
    ncore = lax.axis_size("core")
    nrow = lax.axis_size("y") * ncore
    nx, nz = lax.axis_size("x"), lax.axis_size("z")
    ncol = nx * nz
    col = lax.axis_index(COL)
    halves = rows // cols
    piece = cols // nrow
    own_rows = rows // ncol
    slot = width // ncol
    i32 = lambda *shape: jax.ShapeDtypeStruct(shape, jnp.int32)
    f32 = lambda *shape: jax.ShapeDtypeStruct(shape, jnp.float32)

    pairs = []
    for s in range(nrow):
        for q in range(ncol):
            r, h = q // halves, q % halves
            pairs.append((s * ncol + q, r * ncol + halves * s + h))
    to_row = col // halves
    at = (col % halves) * nrow + (to_row % ncore) * (nrow // ncore) + to_row // ncore
    sent = pl.pallas_call(
        piece_kernel,
        out_shape=pltpu.VMEM((piece, 2 * width), jnp.bfloat16),
        grid_spec=pltpu.PrefetchScalarGridSpec(
            num_scalar_prefetch=2,
            grid=(1,),
            in_specs=[pl.BlockSpec((2, piece, width), lambda i, at, mask: (0, at[0], 0))],
            out_specs=VMEM,
        ),
        name="piece",
    )(at.reshape(1), panel_mask, factor)
    mine = lax.ppermute(sent, ROW + COL, pairs)
    same = lax.all_to_all(
        jnp.broadcast_to(mine[None], (nrow // ncore,) + mine.shape), "y", 0, 0, tiled=True
    ).reshape(cols // ncore, 2 * width)
    other = lax.ppermute(same, "core", [(0, 1), (1, 0)])

    coded = call(
        product_kernel,
        i32(nx, nz * slot, rows + 128),
        smem=2,
        scratch=[pltpu.VMEM((2 * width, cols), jnp.bfloat16), pltpu.VMEM((2 * width, rows), jnp.float32)],
        name="product",
    )(tile_mask, lax.axis_index("core").reshape(1), same, other, inverse_block)
    coded = lax.all_to_all(coded, "x", 0, 0, tiled=True)
    coded = call(middle_kernel, i32(nz * slot, rows + 128), name="middle")(coded)
    coded = lax.all_to_all(coded.reshape(nz, slot, rows + 128), "z", 0, 0, tiled=True)
    gram, total = call(
        gram_kernel, (i32(nrow, 3 * slot + 8, width // 2), f32(2, slot, rows)), smem=1, name="gram"
    )(panel_mask, coded, factor)
    gram = lax.all_to_all(gram, ROW, 0, 0, tiled=True)

    row_step, row_code = scale_of(jnp.max(jnp.abs(total)))
    fixed = whole(total, FIXED / row_step)
    fixed = fixed.reshape(2, slot // 2, 2, nx, nz, own_rows).transpose(3, 4, 1, 2, 0, 5)
    fixed = fixed.reshape(ncol, slot // 2, 128)
    last = call(spread_kernel, i32(ncol, 3 * slot + 8, width // 2), name="spread")(
        gram, fixed, jnp.broadcast_to(row_code, (1, 128))
    )
    last = lax.all_to_all(last, COL, 0, 0, tiled=True)
    return tuple(
        call(
            final_kernel,
            (f32(own_rows, width), f32(width, width), f32(width, width), f32(own_rows, width), f32(width, width)),
            results=None,
            name="final",
        )(last, child_top, pivots)
    )


def solution(mesh):
    grid = Mesh(mesh.devices.reshape(8, 2, 4, 8), ROW + COL)
    in_specs = (P(ROW, COL), P(ROW, COL), P(None, ROW, None), P(None, ROW), P(), P())
    out_specs = (P(ROW + COL, None), P(), P(), P(ROW + COL, None), P())
    return jax.shard_map(shards, mesh=grid, in_specs=in_specs, out_specs=out_specs, check_vma=False)
```

time: 138 us -> 125 us (0.906); the launches traced: 135 us -> 125 us
  blocking collectives: 22.5 us -> 80.4 us
  waiting for transfers between devices: 52.3 us -> 11.7 us
  starting transfers between devices: 39.3 us -> 21.1 us
  Pallas kernels: 0 us -> 8.07 us
  other arithmetic: 8.64 us -> 0.61 us
  local copies, waits for them, and re-layouts: 6.92 us -> 1.29 us
  matrix products: 3.66 us -> 0 us
    all_to_all x1 -> x4, blocking collectives: 22.5 us -> 80.4 us  [the longest x1 22.5 us: shards(): lax.all_to_all(jnp.broadcast_to(mine[None], (nrow // ncore,) + mine.shape...]
    all_to_all x4 -> x1, waiting for transfers between devices: 49.5 us -> 9.7 us  [shards(): gram = lax.all_to_all(gram, ROW, 0, 0, tiled=True)]
    all_to_all x4 -> x1, starting transfers between devices: 20 us -> 6.37 us  [shards(): gram = lax.all_to_all(gram, ROW, 0, 0, tiled=True)]
    pallas_call x0 -> x6, Pallas kernels: none -> 8.07 us  [the longest x5 6.49 us: run(): pl.pallas_call(kernel, out_shape=shapes, in_specs=[SMEM] * smem + [VMEM]...]
    ppermute x1 -> x0, starting transfers between devices: 4.62 us -> none  [shards(): gram = gram + lax.ppermute(gram, 'core', [(0, 1), (1, 0)])]
    dot_general x7 -> x0, matrix products: 3.66 us -> none  [the longest x6 2.79 us: mm(): lax.dot_general(a, b, (((ca,), (cb,)), ((), ())), precision=HIGHEST, pref...]
    concatenate x6 -> x0, other arithmetic: 2.77 us -> none  [the longest x2 1.83 us: exchange(): jnp.concatenate([body, code], axis=2)]
    unnamed x18 -> x11, local copies, waits for them, and re-layouts: 3.01 us -> 0.7 us
  transfers between devices with their start and end apart: 7 -> 3, of which waited for: 7 -> 3; matrix products, arithmetic and copies ran while one was open for 2% -> 1% of each run, Pallas kernels for 0% -> 0%
where the time goes in v2:
time: 125 us
  blocking collectives  80.4 us (64%)
  starting transfers between devices  21.1 us (17%)
  waiting for transfers between devices  11.7 us (9%)
  Pallas kernels  8.07 us (6%)
  between operations  1.61 us (1%)
  local copies, waits for them, and re-layouts  1.29 us (1%)
    all_to_all x1, blocking collectives, shards(): lax.all_to_all(jnp.broadcast_to(mine[None], (nrow // ncore,) + mine.shape...  22.5 us
    all_to_all x1, blocking collectives, shards(): last = lax.all_to_all(last, COL, 0, 0, tiled=True)  19.8 us
    all_to_all x1, blocking collectives, shards(): lax.all_to_all(coded.reshape(nz, slot, rows + 128), 'z', 0, 0, tiled=True)  19.7 us
    all_to_all x1, blocking collectives, shards(): coded = lax.all_to_all(coded, 'x', 0, 0, tiled=True)  18.4 us
    all_to_all x1, waiting for transfers between devices, shards(): gram = lax.all_to_all(gram, ROW, 0, 0, tiled=True)  9.7 us
    ppermute x1, starting transfers between devices, shards(): other = lax.ppermute(same, 'core', [(0, 1), (1, 0)])  7.53 us
    ppermute x1, starting transfers between devices, shards(): mine = lax.ppermute(sent, ROW + COL, pairs)  7.18 us
    pallas_call x5, Pallas kernels, run(): pl.pallas_call(kernel, out_shape=shapes, in_specs=[SMEM] * smem + [VMEM]...  6.49 us
  transfers between devices with their start and end apart: 3, of which 3 were waited for; matrix products, arithmetic and copies ran while one was open for 1% of the time, Pallas kernels for 0%

profile of v2, /device:TPU:1, one launch (start us, length us, event | category | flops | bytes accessed | tf_op | source)
XLA Modules:
  0.0 124.8 jit_solution(15345391077448449108)
XLA Ops:
  0.6 0.0 copy-start.4
  0.6 0.0 copy-start.1
  0.7 1.6 %piece.1 = bf16[32,512]{1,0:T(8,128)(2,1)S(1)} custom-call(s32[1]{0:T(128)} %bitcast.1.at_ref, s32[2,8]{1,0:T(2,128)} %mask_ref.4, bf16[2,1024,256]{2,1,0:T(8,128)(2,1)} %factor_ref.3), custom_call_target="tpu_custom_call" | custom-call | tf_op jit(solution)/shard_map/piece/pallas_call | solution.py:270
  2.3 7.2 %collective-permute-start = (bf16[32,512]{1,0:T(8,128)(2,1)S(1)}, bf16[32,512]{1,0:T(8,128)(2,1)S(1)}, u32[]{:S(2)}, u32[]{:S(2)}) collective-permute-start(bf16[32,512]{1,0:T(8,128)(2,1)S(1)} %piece.1), channel_id=1, source_target_pairs={{0,0},{1,1},{2,32},{3,33},{4,64},{5,65},{6,96},{7,97},{8,128},{9,1... | collective-permute-start | bytes 98312 | tf_op jit(solution)/shard_map/ppermute | solution.py:281
  9.5 1.6 %collective-permute-done = bf16[32,512]{1,0:T(8,128)(2,1)S(1)} collective-permute-done((bf16[32,512]{1,0:T(8,128)(2,1)S(1)}, bf16[32,512]{1,0:T(8,128)(2,1)S(1)}, u32[]{:S(2)}, u32[]{:S(2)}) %collective-permute-start) | collective-permute-done | bytes 32800 | tf_op jit(solution)/shard_map/ppermute | solution.py:281
  11.1 22.5 %all_to_all.25 = bf16[8,32,512]{2,1,0:T(8,128)(2,1)S(1)} all-to-all(bf16[8,32,512]{2,1,0:T(8,128)(2,1)S(1)} %broadcast_in_dim.4), channel_id=1, replica_groups=mesh['y'=8,'core'=2,'x'=4,'z'=8] {'y'}, dimensions={0} | all-to-all | bytes 524288 | tf_op jit(solution)/shard_map/all_to_all | solution.py:282
  33.5 7.5 %collective-permute-start.1 = (bf16[256,512]{1,0:T(8,128)(2,1)S(1)}, bf16[256,512]{1,0:T(8,128)(2,1)S(1)}, u32[]{:S(2)}, u32[]{:S(2)}) collective-permute-start(bf16[256,512]{1,0:T(8,128)(2,1)S(1)} %bitcast.8), channel_id=1, source_target_pairs={{0,32},{32,0},{1,33},{33,1},{2,34},{34,2},{3,35},{35,3},{4,36},{36... | collective-permute-start | bytes 786440 | tf_op jit(solution)/shard_map/ppermute | solution.py:285
  41.1 0.0 copy-done.4
  41.1 0.7 copy.11.mask_ref
  41.8 0.5 collective-permute-done.1.other_ref
  42.2 0.0 copy-done.1
  42.2 1.9 %product.1 = s32[4,64,1152]{2,1,0:T(8,128)S(1)} custom-call(s32[8,4]{1,0:T(8,128)} %copy.11.mask_ref, s32[1]{0:T(128)} %bitcast.core_ref, bf16[256,512]{1,0:T(8,128)(2,1)S(1)} %bitcast.9, bf16[256,512]{1,0:T(8,128)(2,1)S(1)} %collective-permute-done.1.other_ref, bf16[1024,512]{1,0:T(8,128)(2,1)S(1)} %copy-done.1), custom_call_target="tpu_custom_call" | custom-call | tf_op jit(solution)/shard_map/product/pallas_call | solution.py:235
  44.1 18.4 %all_to_all.26.in_ref = s32[4,64,1152]{2,1,0:T(8,128)S(1)} all-to-all(s32[4,64,1152]{2,1,0:T(8,128)S(1)} %product.1), channel_id=1, replica_groups=mesh['y'=8,'core'=2,'x'=4,'z'=8] {'x'}, dimensions={0} | all-to-all | bytes 2359296 | tf_op jit(solution)/shard_map/all_to_all | solution.py:294
  62.5 0.0 copy-start
  62.5 0.5 middle.1
  62.9 19.7 %all_to_all.27.in_ref = s32[8,8,1152]{2,1,0:T(8,128)S(1)} all-to-all(s32[8,8,1152]{2,1,0:T(8,128)S(1)} %bitcast.7), channel_id=1, replica_groups=mesh['y'=8,'core'=2,'x'=4,'z'=8] {'z'}, dimensions={0} | all-to-all | bytes 589824 | tf_op jit(solution)/shard_map/all_to_all | solution.py:296
  82.7 0.0 copy-done
  82.7 2.0 %gram.1 = (s32[16,32,128]{2,1,0:T(8,128)}, f32[2,8,1024]{2,1,0:T(8,128)S(1)}) custom-call(s32[2,8]{1,0:T(2,128)} %mask_ref.4, s32[8,8,1152]{2,1,0:T(8,128)S(1)} %all_to_all.27.in_ref, bf16[2,1024,256]{2,1,0:T(8,128)(2,1)S(1)} %copy-done), custom_call_target="tpu_custom_call" | custom-call | tf_op jit(solution)/shard_map/gram/pallas_call | solution.py:235
  84.6 6.4 %all-to-all-start.3 = ((s32[16,32,128]{2,1,0:T(8,128)}), s32[16,32,128]{2,1,0:T(8,128)S(1)}, u32[]{:S(2)}, u32[]{:S(2)}) async-start(s32[16,32,128]{2,1,0:T(8,128)} %get-tuple-element.7), calls=%async_computation.3 | async-start | bytes 524288 | tf_op jit(solution)/shard_map/all_to_all | solution.py:300
  91.0 0.6 abs_reduce_fusion
  92.4 0.1 reshape.33
  92.5 0.2 copy.14
  92.8 0.0 copy-start.2
  92.8 0.0 copy-start.3
  92.8 0.3 reshape.34.fixed_ref
  93.0 9.7 %all-to-all-done.3.in_ref = s32[16,32,128]{2,1,0:T(8,128)S(1)} async-done(((s32[16,32,128]{2,1,0:T(8,128)}), s32[16,32,128]{2,1,0:T(8,128)S(1)}, u32[]{:S(2)}, u32[]{:S(2)}) %all-to-all-start.3) | async-done | bytes 262176 | tf_op jit(solution)/shard_map/all_to_all | solution.py:300
  102.7 0.3 spread.1
  103.0 19.8 %all_to_all.28.in_ref = s32[32,32,128]{2,1,0:T(8,128)S(1)} all-to-all(s32[32,32,128]{2,1,0:T(8,128)S(1)} %spread.1), channel_id=1, replica_groups=mesh['y'=8,'core'=2,'x'=4,'z'=8] {'x','z'}, dimensions={0} | all-to-all | bytes 1048576 | tf_op jit(solution)/shard_map/all_to_all | solution.py:309
  122.9 0.0 copy-done.2
  122.9 0.0 copy-done.3
  122.9 1.9 %final.1 = (f32[32,256]{1,0:T(8,128)}, f32[256,256]{1,0:T(8,128)}, f32[256,256]{1,0:T(8,128)}, f32[32,256]{1,0:T(8,128)}, f32[256,256]{1,0:T(8,128)}) custom-call(s32[32,32,128]{2,1,0:T(8,128)S(1)} %all_to_all.28.in_ref, bf16[256,256]{1,0:T(8,128)(2,1)S(1)} %copy-done.3, f32[2,256,256]{2,1,0:T(8,128)S(1)} %copy-done.2), custom_call_target="tpu_custom_call" | custom-call | tf_op jit(solution)/shard_map/final/pallas_call | solution.py:235
  (3 shorter events, 0.0 us)
Async XLA Ops:
  0.6 40.5 %copy-start.4 = (s32[8,4]{0,1:T(4,128)S(1)}, s32[8,4]{0,1:T(4,128)}, u32[]{:S(2)}) copy-start(s32[8,4]{0,1:T(4,128)} %param.7) | copy-start | bytes 388
  0.6 41.6 %copy-start.1 = (bf16[1024,512]{1,0:T(8,128)(2,1)S(1)}, bf16[1024,512]{1,0:T(8,128)(2,1)}, u32[]{:S(2)}) copy-start(bf16[1024,512]{1,0:T(8,128)(2,1)} %inverse_ref.1) | copy-start | bytes 3145732
  2.3 8.8 %collective-permute-start = (bf16[32,512]{1,0:T(8,128)(2,1)S(1)}, bf16[32,512]{1,0:T(8,128)(2,1)S(1)}, u32[]{:S(2)}, u32[]{:S(2)}) collective-permute-start(bf16[32,512]{1,0:T(8,128)(2,1)S(1)} %piece.1), channel_id=1, source_target_pairs={{0,0},{1,1},{2,32},{3,33},{4,64},{5,65},{6,96},{7,97},{8,128},{9,1... | collective-permute-start | bytes 98312 | tf_op jit(solution)/shard_map/ppermute | solution.py:281
  33.5 8.7 %collective-permute-start.1 = (bf16[256,512]{1,0:T(8,128)(2,1)S(1)}, bf16[256,512]{1,0:T(8,128)(2,1)S(1)}, u32[]{:S(2)}, u32[]{:S(2)}) collective-permute-start(bf16[256,512]{1,0:T(8,128)(2,1)S(1)} %bitcast.8), channel_id=1, source_target_pairs={{0,32},{32,0},{1,33},{33,1},{2,34},{34,2},{3,35},{35,3},{4,36},{36... | collective-permute-start | bytes 786440 | tf_op jit(solution)/shard_map/ppermute | solution.py:285
  62.5 20.2 %copy-start = (bf16[2,1024,256]{2,1,0:T(8,128)(2,1)S(1)}, bf16[2,1024,256]{2,1,0:T(8,128)(2,1)}, u32[]{:S(2)}) copy-start(bf16[2,1024,256]{2,1,0:T(8,128)(2,1)} %factor_ref.3) | copy-start | bytes 3145732
  84.6 18.1 %all-to-all-start.3 = ((s32[16,32,128]{2,1,0:T(8,128)}), s32[16,32,128]{2,1,0:T(8,128)S(1)}, u32[]{:S(2)}, u32[]{:S(2)}) async-start(s32[16,32,128]{2,1,0:T(8,128)} %get-tuple-element.7), calls=%async_computation.3 | async-start | bytes 524288 | tf_op jit(solution)/shard_map/all_to_all | solution.py:300
  92.8 30.1 %copy-start.2 = (f32[2,256,256]{2,1,0:T(8,128)S(1)}, f32[2,256,256]{2,1,0:T(8,128)}, u32[]{:S(2)}) copy-start(f32[2,256,256]{2,1,0:T(8,128)} %pivots_ref.1) | copy-start | bytes 1572868
  92.8 30.1 %copy-start.3 = (bf16[256,256]{1,0:T(8,128)(2,1)S(1)}, bf16[256,256]{1,0:T(8,128)(2,1)}, u32[]{:S(2)}) copy-start(bf16[256,256]{1,0:T(8,128)(2,1)} %top_ref.1) | copy-start | bytes 393220

commit v3 on v2

--- a/solution.py
+++ b/solution.py
@@ -62,12 +62,43 @@
     return high * (scale_from(code[:, :1]) * (1.0 / LIMIT)), low * (scale_from(code[:, 64:65]) * (1.0 / LIMIT))
 
 
-def piece_kernel(at_ref, mask_ref, factor_ref, out_ref):
-    width = factor_ref.shape[2]
-    block = at_ref[0] * factor_ref.shape[1] // 128
+SERVES = [
+    [18, 23, 17, 15, 5, 0, 24, 22, 20, 21, 8, 11, 7, 4, 31, 12, 14, 13, 9, 29, 3, 2, 28, 10, 16, 19, 27, 25, 1, 6, 30, 26],
+    [22, 16, 8, 21, 25, 13, 11, 4, 6, 14, 20, 19, 29, 5, 3, 30, 28, 26, 12, 15, 9, 31, 1, 0, 10, 24, 18, 17, 23, 27, 7, 2],
+    [29, 12, 18, 26, 22, 19, 21, 13, 11, 8, 14, 24, 28, 25, 17, 1, 7, 6, 2, 10, 9, 27, 31, 4, 5, 0, 30, 16, 20, 23, 15, 3],
+    [13, 3, 29, 10, 16, 26, 19, 21, 17, 1, 5, 4, 18, 14, 22, 27, 15, 11, 7, 6, 2, 12, 20, 25, 31, 8, 9, 0, 28, 30, 24, 23],
+    [24, 27, 3, 13, 9, 12, 2, 30, 26, 25, 23, 17, 1, 18, 0, 8, 20, 29, 21, 19, 15, 6, 14, 28, 22, 31, 5, 11, 7, 10, 4, 16],
+    [2, 6, 24, 27, 1, 5, 13, 10, 0, 26, 25, 28, 23, 29, 14, 16, 7, 22, 30, 3, 21, 19, 9, 12, 4, 18, 20, 31, 17, 15, 11, 8],
+    [11, 8, 4, 2, 28, 29, 1, 5, 9, 16, 6, 26, 30, 25, 31, 7, 13, 10, 22, 0, 14, 27, 21, 17, 15, 12, 18, 20, 24, 3, 23, 19],
+    [25, 5, 9, 14, 4, 6, 30, 29, 23, 3, 13, 10, 11, 28, 2, 31, 27, 21, 17, 18, 20, 22, 0, 26, 7, 19, 15, 12, 8, 24, 16, 1],
+    [30, 3, 23, 25, 19, 18, 14, 8, 2, 7, 29, 13, 17, 20, 10, 6, 4, 5, 31, 27, 11, 16, 22, 26, 0, 9, 1, 21, 15, 12, 24, 28],
+    [14, 24, 30, 7, 25, 23, 17, 16, 10, 2, 12, 31, 11, 9, 15, 22, 26, 0, 4, 1, 5, 29, 13, 8, 18, 28, 6, 3, 27, 21, 19, 20],
+    [23, 22, 26, 18, 10, 11, 25, 19, 21, 20, 14, 2, 4, 13, 17, 15, 31, 12, 16, 30, 6, 5, 7, 9, 27, 24, 28, 8, 0, 3, 1, 29],
+    [13, 19, 21, 20, 24, 28, 10, 3, 15, 16, 25, 22, 14, 0, 4, 5, 11, 29, 27, 12, 30, 9, 6, 2, 1, 31, 17, 26, 18, 23, 8, 7],
+    [8, 15, 7, 1, 31, 22, 28, 16, 4, 20, 3, 21, 25, 26, 24, 0, 10, 9, 13, 5, 23, 27, 18, 6, 14, 11, 30, 19, 29, 2, 17, 12],
+    [28, 0, 12, 9, 13, 3, 29, 24, 20, 6, 4, 7, 17, 21, 25, 26, 2, 18, 8, 15, 5, 19, 27, 22, 30, 14, 16, 10, 11, 31, 1, 23],
+    [3, 31, 2, 4, 14, 17, 5, 24, 29, 30, 0, 18, 8, 9, 7, 27, 1, 28, 26, 20, 16, 15, 19, 23, 25, 6, 10, 22, 12, 13, 21, 11],
+    [19, 5, 25, 29, 0, 8, 4, 11, 7, 27, 31, 30, 24, 2, 18, 9, 17, 21, 1, 26, 28, 10, 14, 13, 22, 3, 23, 6, 20, 16, 12, 15],
+]
+
+
+def plan(ncore, ncol):
+    pairs, pieces = [], []
+    for s, line in enumerate(SERVES):
+        for q, target in enumerate(line):
+            r, h = divmod(target, 2)
+            pairs.append((s * ncol + q, r * ncol + 2 * s + h))
+            pieces.append(h * ncore + r % ncore)
+    return pairs, pieces
+
+
+def piece_kernel(device_ref, at_ref, mask_ref, factor_ref, out_ref):
+    rows, width = factor_ref.shape[1:]
+    block = at_ref[device_ref[0]] * (rows // 128)
     for k in range(2):
-        kept = jnp.where(mask_ref[k, block] == 1, factor_ref[k], 0.0)
-        out_ref[:, k * width : k * width + width] = kept.astype(jnp.bfloat16)
+        for i in range(rows // 128):
+            kept = jnp.where(mask_ref[k, block + i] == 1, factor_ref[k, i * 128 : i * 128 + 128, :], 0.0)
+            out_ref[i * 128 : i * 128 + 128, k * width : k * width + width] = kept.astype(jnp.bfloat16)
 
 
 def product_kernel(mask_ref, core_ref, same_ref, other_ref, inverse_ref, out_ref, turned, product):
@@ -121,14 +152,31 @@
         store(k, join(whole(gram[:, :half], inverse), whole(gram[:, half:], inverse)), code)
 
 
-def gram_kernel(mask_ref, in_ref, factor_ref, out_ref, total_ref):
+def place_rows(high, low, fixed_ref, code_ref):
+    top = jnp.max(jnp.maximum(jnp.abs(high), jnp.abs(low)), axis=1, keepdims=True)
+    step, code = scale_of(jnp.broadcast_to(jnp.max(top, axis=0, keepdims=True), (1, 128)))
+    code_ref[...] = code
+    inverse = (FIXED / step)[:, :1]
+    parts = [whole(v, inverse)[h * 4 : h * 4 + 4] for h in range(2) for v in (high, low)]
+    lane = lax.broadcasted_iota(jnp.int32, (4, 128), 1) // 32
+    for tile in range(high.shape[1] // 128):
+        pieces = [p[:, tile * 128 : tile * 128 + 128] for p in parts]
+        turned = [[p if s == 0 else pltpu.roll(p, 32 * s, 1) for s in range(4)] for p in pieces]
+        for quarter in range(4):
+            found = turned[0][-quarter % 4]
+            for b in range(1, 4):
+                found = jnp.where(lane == b, turned[b][(b - quarter) % 4], found)
+            fixed_ref[tile * 4 + quarter] = found
+
+
+def gram_kernel(mask_ref, in_ref, factor_ref, out_ref, fixed_ref, code_ref):
     rows = in_ref.shape[2] - 128
     slot = in_ref.shape[1]
     high, low = decode_rows(in_ref, 0, rows)
     for i in range(1, in_ref.shape[0]):
         more_high, more_low = decode_rows(in_ref, i, rows)
         high, low = high + more_high, low + more_low
-    total_ref[0], total_ref[1] = high, low
+    place_rows(high, low, fixed_ref, code_ref)
     pieces = jnp.concatenate([p.astype(jnp.float32) for p in split(high) + split(low)], axis=0)
     pieces = pieces.astype(jnp.bfloat16)
     sums = []
@@ -216,7 +264,7 @@
     column = lax.broadcasted_iota(jnp.int32, (count, width), 1)
     placed = None
     for h in range(2):
-        choice = jnp.where(column == 2 * row + h, 1.0, 0.0).astype(jnp.bfloat16)
+        choice = jnp.where(column == slot * (row // 4) + 4 * h + row % 4, 1.0, 0.0).astype(jnp.bfloat16)
         for piece in split(sums):
             term = dot(piece, choice, 0, 0)[64 * h : 64 * h + 64]
             placed = term if placed is None else placed + term
@@ -252,36 +300,25 @@
     nrow = lax.axis_size("y") * ncore
     nx, nz = lax.axis_size("x"), lax.axis_size("z")
     ncol = nx * nz
-    col = lax.axis_index(COL)
-    halves = rows // cols
-    piece = cols // nrow
+    piece = cols // ncore
     own_rows = rows // ncol
     slot = width // ncol
     i32 = lambda *shape: jax.ShapeDtypeStruct(shape, jnp.int32)
     f32 = lambda *shape: jax.ShapeDtypeStruct(shape, jnp.float32)
 
-    pairs = []
-    for s in range(nrow):
-        for q in range(ncol):
-            r, h = q // halves, q % halves
-            pairs.append((s * ncol + q, r * ncol + halves * s + h))
-    to_row = col // halves
-    at = (col % halves) * nrow + (to_row % ncore) * (nrow // ncore) + to_row // ncore
+    pairs, pieces = plan(ncore, ncol)
     sent = pl.pallas_call(
         piece_kernel,
         out_shape=pltpu.VMEM((piece, 2 * width), jnp.bfloat16),
         grid_spec=pltpu.PrefetchScalarGridSpec(
-            num_scalar_prefetch=2,
+            num_scalar_prefetch=3,
             grid=(1,),
-            in_specs=[pl.BlockSpec((2, piece, width), lambda i, at, mask: (0, at[0], 0))],
+            in_specs=[pl.BlockSpec((2, piece, width), lambda i, device, at, mask: (0, at[device[0]], 0))],
             out_specs=VMEM,
         ),
         name="piece",
-    )(at.reshape(1), panel_mask, factor)
-    mine = lax.ppermute(sent, ROW + COL, pairs)
-    same = lax.all_to_all(
-        jnp.broadcast_to(mine[None], (nrow // ncore,) + mine.shape), "y", 0, 0, tiled=True
-    ).reshape(cols // ncore, 2 * width)
+    )(lax.axis_index(ROW + COL).reshape(1), jnp.array(pieces, jnp.int32), panel_mask, factor)
+    same = lax.ppermute(sent, ROW + COL, pairs)
     other = lax.ppermute(same, "core", [(0, 1), (1, 0)])
 
     coded = call(
@@ -294,17 +331,16 @@
     coded = lax.all_to_all(coded, "x", 0, 0, tiled=True)
     coded = call(middle_kernel, i32(nz * slot, rows + 128), name="middle")(coded)
     coded = lax.all_to_all(coded.reshape(nz, slot, rows + 128), "z", 0, 0, tiled=True)
-    gram, total = call(
-        gram_kernel, (i32(nrow, 3 * slot + 8, width // 2), f32(2, slot, rows)), smem=1, name="gram"
+    gram, fixed, code = call(
+        gram_kernel,
+        (i32(nrow, 3 * slot + 8, width // 2), i32(ncol, slot // 2, 128), i32(1, 128)),
+        smem=1,
+        name="gram",
     )(panel_mask, coded, factor)
     gram = lax.all_to_all(gram, ROW, 0, 0, tiled=True)
 
-    row_step, row_code = scale_of(jnp.max(jnp.abs(total)))
-    fixed = whole(total, FIXED / row_step)
-    fixed = fixed.reshape(2, slot // 2, 2, nx, nz, own_rows).transpose(3, 4, 1, 2, 0, 5)
-    fixed = fixed.reshape(ncol, slot // 2, 128)
     last = call(spread_kernel, i32(ncol, 3 * slot + 8, width // 2), name="spread")(
-        gram, fixed, jnp.broadcast_to(row_code, (1, 128))
+        gram, fixed, code
     )
     last = lax.all_to_all(last, COL, 0, 0, tiled=True)
     return tuple(

time: 125 us -> 115 us (0.920)
  starting transfers between devices: 21.1 us -> 13 us
    all_to_all x1 -> x0, waiting for transfers between devices: 9.7 us -> none  [shards(): gram = lax.all_to_all(gram, ROW, 0, 0, tiled=True)]
    ppermute x1, waiting for transfers between devices: 1.58 us -> 10.2 us  [shards(): same = lax.ppermute(sent, ROW + COL, pairs)]
    all_to_all x1, blocking collectives: 19.7 us -> 12.9 us  [shards(): lax.all_to_all(coded.reshape(nz, slot, rows + 128), 'z', 0, 0, tiled=True)]
    all_to_all x1 -> x0, starting transfers between devices: 6.37 us -> none  [shards(): gram = lax.all_to_all(gram, ROW, 0, 0, tiled=True)]
    ppermute x1, starting transfers between devices: 7.53 us -> 1.91 us  [shards(): other = lax.ppermute(same, 'core', [(0, 1), (1, 0)])]
    all_to_all x1, blocking collectives: 18.4 us -> 23.9 us  [shards(): coded = lax.all_to_all(coded, 'x', 0, 0, tiled=True)]
    ppermute x1, starting transfers between devices: 7.18 us -> 11.1 us  [shards(): same = lax.ppermute(sent, ROW + COL, pairs)]
    all_to_all x1, blocking collectives: 22.5 us -> 24.3 us  [shards(): gram = lax.all_to_all(gram, ROW, 0, 0, tiled=True)]
  transfers between devices with their start and end apart: 3 -> 2, of which waited for: 3 -> 2; matrix products, arithmetic and copies ran while one was open for 1% -> 1% of each run, Pallas kernels for 0% -> 0%
where the time goes in v3:
time: 115 us; the launch traced here: 114 us
  blocking collectives  81.1 us (71%)
  starting transfers between devices  13 us (11%)
  waiting for transfers between devices  11 us (10%)
  Pallas kernels  7.61 us (7%)
    all_to_all x1, blocking collectives, shards(): gram = lax.all_to_all(gram, ROW, 0, 0, tiled=True)  24.3 us
    all_to_all x1, blocking collectives, shards(): coded = lax.all_to_all(coded, 'x', 0, 0, tiled=True)  23.9 us
    all_to_all x1, blocking collectives, shards(): last = lax.all_to_all(last, COL, 0, 0, tiled=True)  19.9 us
    all_to_all x1, blocking collectives, shards(): lax.all_to_all(coded.reshape(nz, slot, rows + 128), 'z', 0, 0, tiled=True)  12.9 us
    ppermute x1, starting transfers between devices, shards(): same = lax.ppermute(sent, ROW + COL, pairs)  11.1 us
    ppermute x1, waiting for transfers between devices, shards(): same = lax.ppermute(sent, ROW + COL, pairs)  10.2 us
    pallas_call x5, Pallas kernels, run(): pl.pallas_call(kernel, out_shape=shapes, in_specs=[SMEM] * smem + [VMEM]...  5.78 us
  transfers between devices with their start and end apart: 2, of which 2 were waited for; matrix products, arithmetic and copies ran while one was open for 1% of the time, Pallas kernels for 0%

profile of v3, /device:TPU:1, one launch (start us, length us, event | category | flops | bytes accessed | tf_op | source)
XLA Modules:
  0.0 114.2 jit_solution(13118731617424136123)
XLA Ops:
  0.6 0.0 copy-start.4
  0.6 0.0 copy-start.1
  0.7 1.8 %piece.1 = bf16[256,512]{1,0:T(8,128)(2,1)S(1)} custom-call(s32[1]{0:T(128)} %bitcast.1.device_ref, s32[512]{0:T(512)} %constant.26.clone.at_ref, s32[2,8]{1,0:T(2,128)} %mask_ref.4, bf16[2,1024,256]{2,1,0:T(8,128)(2,1)} %factor_ref.3), custom_call_target="tpu_custom_call" | custom-call | tf_op jit(solution)/shard_map/piece/pallas_call | solution.py:310
  2.5 11.1 %collective-permute-start = (bf16[256,512]{1,0:T(8,128)(2,1)S(1)}, bf16[256,512]{1,0:T(8,128)(2,1)S(1)}, u32[]{:S(2)}, u32[]{:S(2)}) collective-permute-start(bf16[256,512]{1,0:T(8,128)(2,1)S(1)} %piece.1), channel_id=1, source_target_pairs={{0,288},{1,353},{2,257},{3,225},{4,65},{5,0},{6,384},{7,352},{8,32... | collective-permute-start | bytes 786440 | tf_op jit(solution)/shard_map/ppermute | solution.py:321
  13.6 10.2 %collective-permute-done.same_ref = bf16[256,512]{1,0:T(8,128)(2,1)S(1)} collective-permute-done((bf16[256,512]{1,0:T(8,128)(2,1)S(1)}, bf16[256,512]{1,0:T(8,128)(2,1)S(1)}, u32[]{:S(2)}, u32[]{:S(2)}) %collective-permute-start) | collective-permute-done | bytes 262176 | tf_op jit(solution)/shard_map/ppermute | solution.py:321
  23.8 1.9 %collective-permute-start.1 = (bf16[256,512]{1,0:T(8,128)(2,1)S(1)}, bf16[256,512]{1,0:T(8,128)(2,1)S(1)}, u32[]{:S(2)}, u32[]{:S(2)}) collective-permute-start(bf16[256,512]{1,0:T(8,128)(2,1)S(1)} %collective-permute-done.same_ref), channel_id=1, source_target_pairs={{0,32},{32,0},{1,33},{33,1},{2,34},{34,2},{3,35},{35,3},{4,36},{36... | collective-permute-start | bytes 786440 | tf_op jit(solution)/shard_map/ppermute | solution.py:322
  25.8 0.0 copy-done.4
  25.8 0.7 copy.12.mask_ref
  26.4 0.8 collective-permute-done.1.other_ref
  27.3 0.0 copy-done.1
  27.3 1.9 %product.1 = s32[4,64,1152]{2,1,0:T(8,128)S(1)} custom-call(s32[8,4]{1,0:T(8,128)} %copy.12.mask_ref, s32[1]{0:T(128)} %bitcast.core_ref, bf16[256,512]{1,0:T(8,128)(2,1)S(1)} %collective-permute-done.same_ref, bf16[256,512]{1,0:T(8,128)(2,1)S(1)} %collective-permute-done.1.other_ref, bf16[1024,512]{1,0:T(8,128)(2,1)S(1)} %copy-done.1), custom_call_target="tpu_custom_call" | custom-call | tf_op jit(solution)/shard_map/product/pallas_call | solution.py:283
  29.1 23.9 %all_to_all.20.in_ref = s32[4,64,1152]{2,1,0:T(8,128)S(1)} all-to-all(s32[4,64,1152]{2,1,0:T(8,128)S(1)} %product.1), channel_id=1, replica_groups=mesh['y'=8,'core'=2,'x'=4,'z'=8] {'x'}, dimensions={0} | all-to-all | bytes 2359296 | tf_op jit(solution)/shard_map/all_to_all | solution.py:331
  53.1 0.0 copy-start
  53.1 0.5 middle.1
  53.5 12.9 %all_to_all.21.in_ref = s32[8,8,1152]{2,1,0:T(8,128)S(1)} all-to-all(s32[8,8,1152]{2,1,0:T(8,128)S(1)} %bitcast.3), channel_id=1, replica_groups=mesh['y'=8,'core'=2,'x'=4,'z'=8] {'z'}, dimensions={0} | all-to-all | bytes 589824 | tf_op jit(solution)/shard_map/all_to_all | solution.py:333
  66.4 0.0 copy-done
  66.4 1.3 %gram.1 = (s32[16,32,128]{2,1,0:T(8,128)S(1)}, s32[32,4,128]{2,1,0:T(4,128)S(1)}, s32[1,128]{1,0:T(1,128)S(1)}) custom-call(s32[2,8]{1,0:T(2,128)} %mask_ref.4, s32[8,8,1152]{2,1,0:T(8,128)S(1)} %all_to_all.21.in_ref, bf16[2,1024,256]{2,1,0:T(8,128)(2,1)S(1)} %copy-done), custom_call_target="tpu_custom_call" | custom-call | tf_op jit(solution)/shard_map/gram/pallas_call | solution.py:283
  67.7 0.0 copy-start.2
  67.7 0.0 copy-start.3
  67.7 24.3 %all_to_all.22.in_ref = s32[16,32,128]{2,1,0:T(8,128)S(1)} all-to-all(s32[16,32,128]{2,1,0:T(8,128)S(1)} %get-tuple-element.8), channel_id=1, replica_groups=mesh['y'=8,'core'=2,'x'=4,'z'=8] {'y','core'}, dimensions={0} | all-to-all | bytes 524288 | tf_op jit(solution)/shard_map/all_to_all | solution.py:340
  92.1 0.3 spread.1
  92.4 19.9 %all_to_all.23.in_ref = s32[32,32,128]{2,1,0:T(8,128)S(1)} all-to-all(s32[32,32,128]{2,1,0:T(8,128)S(1)} %spread.1), channel_id=1, replica_groups=mesh['y'=8,'core'=2,'x'=4,'z'=8] {'x','z'}, dimensions={0} | all-to-all | bytes 1048576 | tf_op jit(solution)/shard_map/all_to_all | solution.py:345
  112.2 0.0 copy-done.2
  112.2 0.0 copy-done.3
  112.2 1.9 %final.1 = (f32[32,256]{1,0:T(8,128)}, f32[256,256]{1,0:T(8,128)}, f32[256,256]{1,0:T(8,128)}, f32[32,256]{1,0:T(8,128)}, f32[256,256]{1,0:T(8,128)}) custom-call(s32[32,32,128]{2,1,0:T(8,128)S(1)} %all_to_all.23.in_ref, bf16[256,256]{1,0:T(8,128)(2,1)S(1)} %copy-done.3, f32[2,256,256]{2,1,0:T(8,128)S(1)} %copy-done.2), custom_call_target="tpu_custom_call" | custom-call | tf_op jit(solution)/shard_map/final/pallas_call | solution.py:283
Async XLA Ops:
  0.6 25.1 %copy-start.4 = (s32[8,4]{0,1:T(4,128)S(1)}, s32[8,4]{0,1:T(4,128)}, u32[]{:S(2)}) copy-start(s32[8,4]{0,1:T(4,128)} %param.8) | copy-start | bytes 388
  0.6 26.6 %copy-start.1 = (bf16[1024,512]{1,0:T(8,128)(2,1)S(1)}, bf16[1024,512]{1,0:T(8,128)(2,1)}, u32[]{:S(2)}) copy-start(bf16[1024,512]{1,0:T(8,128)(2,1)} %inverse_ref.1) | copy-start | bytes 3145732
  2.5 21.3 %collective-permute-start = (bf16[256,512]{1,0:T(8,128)(2,1)S(1)}, bf16[256,512]{1,0:T(8,128)(2,1)S(1)}, u32[]{:S(2)}, u32[]{:S(2)}) collective-permute-start(bf16[256,512]{1,0:T(8,128)(2,1)S(1)} %piece.1), channel_id=1, source_target_pairs={{0,288},{1,353},{2,257},{3,225},{4,65},{5,0},{6,384},{7,352},{8,32... | collective-permute-start | bytes 786440 | tf_op jit(solution)/shard_map/ppermute | solution.py:321
  23.8 3.4 %collective-permute-start.1 = (bf16[256,512]{1,0:T(8,128)(2,1)S(1)}, bf16[256,512]{1,0:T(8,128)(2,1)S(1)}, u32[]{:S(2)}, u32[]{:S(2)}) collective-permute-start(bf16[256,512]{1,0:T(8,128)(2,1)S(1)} %collective-permute-done.same_ref), channel_id=1, source_target_pairs={{0,32},{32,0},{1,33},{33,1},{2,34},{34,2},{3,35},{35,3},{4,36},{36... | collective-permute-start | bytes 786440 | tf_op jit(solution)/shard_map/ppermute | solution.py:322
  53.1 13.4 %copy-start = (bf16[2,1024,256]{2,1,0:T(8,128)(2,1)S(1)}, bf16[2,1024,256]{2,1,0:T(8,128)(2,1)}, u32[]{:S(2)}) copy-start(bf16[2,1024,256]{2,1,0:T(8,128)(2,1)} %factor_ref.3) | copy-start | bytes 3145732
  67.7 44.6 %copy-start.2 = (f32[2,256,256]{2,1,0:T(8,128)S(1)}, f32[2,256,256]{2,1,0:T(8,128)}, u32[]{:S(2)}) copy-start(f32[2,256,256]{2,1,0:T(8,128)} %pivots_ref.1) | copy-start | bytes 1572868
  67.7 44.5 %copy-start.3 = (bf16[256,256]{1,0:T(8,128)(2,1)S(1)}, bf16[256,256]{1,0:T(8,128)(2,1)}, u32[]{:S(2)}) copy-start(bf16[256,256]{1,0:T(8,128)(2,1)} %top_ref.1) | copy-start | bytes 393220

commit v4 on v3

--- a/solution.py
+++ b/solution.py
@@ -63,22 +63,22 @@
 
 
 SERVES = [
-    [18, 23, 17, 15, 5, 0, 24, 22, 20, 21, 8, 11, 7, 4, 31, 12, 14, 13, 9, 29, 3, 2, 28, 10, 16, 19, 27, 25, 1, 6, 30, 26],
-    [22, 16, 8, 21, 25, 13, 11, 4, 6, 14, 20, 19, 29, 5, 3, 30, 28, 26, 12, 15, 9, 31, 1, 0, 10, 24, 18, 17, 23, 27, 7, 2],
-    [29, 12, 18, 26, 22, 19, 21, 13, 11, 8, 14, 24, 28, 25, 17, 1, 7, 6, 2, 10, 9, 27, 31, 4, 5, 0, 30, 16, 20, 23, 15, 3],
-    [13, 3, 29, 10, 16, 26, 19, 21, 17, 1, 5, 4, 18, 14, 22, 27, 15, 11, 7, 6, 2, 12, 20, 25, 31, 8, 9, 0, 28, 30, 24, 23],
-    [24, 27, 3, 13, 9, 12, 2, 30, 26, 25, 23, 17, 1, 18, 0, 8, 20, 29, 21, 19, 15, 6, 14, 28, 22, 31, 5, 11, 7, 10, 4, 16],
-    [2, 6, 24, 27, 1, 5, 13, 10, 0, 26, 25, 28, 23, 29, 14, 16, 7, 22, 30, 3, 21, 19, 9, 12, 4, 18, 20, 31, 17, 15, 11, 8],
-    [11, 8, 4, 2, 28, 29, 1, 5, 9, 16, 6, 26, 30, 25, 31, 7, 13, 10, 22, 0, 14, 27, 21, 17, 15, 12, 18, 20, 24, 3, 23, 19],
-    [25, 5, 9, 14, 4, 6, 30, 29, 23, 3, 13, 10, 11, 28, 2, 31, 27, 21, 17, 18, 20, 22, 0, 26, 7, 19, 15, 12, 8, 24, 16, 1],
-    [30, 3, 23, 25, 19, 18, 14, 8, 2, 7, 29, 13, 17, 20, 10, 6, 4, 5, 31, 27, 11, 16, 22, 26, 0, 9, 1, 21, 15, 12, 24, 28],
-    [14, 24, 30, 7, 25, 23, 17, 16, 10, 2, 12, 31, 11, 9, 15, 22, 26, 0, 4, 1, 5, 29, 13, 8, 18, 28, 6, 3, 27, 21, 19, 20],
-    [23, 22, 26, 18, 10, 11, 25, 19, 21, 20, 14, 2, 4, 13, 17, 15, 31, 12, 16, 30, 6, 5, 7, 9, 27, 24, 28, 8, 0, 3, 1, 29],
-    [13, 19, 21, 20, 24, 28, 10, 3, 15, 16, 25, 22, 14, 0, 4, 5, 11, 29, 27, 12, 30, 9, 6, 2, 1, 31, 17, 26, 18, 23, 8, 7],
-    [8, 15, 7, 1, 31, 22, 28, 16, 4, 20, 3, 21, 25, 26, 24, 0, 10, 9, 13, 5, 23, 27, 18, 6, 14, 11, 30, 19, 29, 2, 17, 12],
-    [28, 0, 12, 9, 13, 3, 29, 24, 20, 6, 4, 7, 17, 21, 25, 26, 2, 18, 8, 15, 5, 19, 27, 22, 30, 14, 16, 10, 11, 31, 1, 23],
-    [3, 31, 2, 4, 14, 17, 5, 24, 29, 30, 0, 18, 8, 9, 7, 27, 1, 28, 26, 20, 16, 15, 19, 23, 25, 6, 10, 22, 12, 13, 21, 11],
-    [19, 5, 25, 29, 0, 8, 4, 11, 7, 27, 31, 30, 24, 2, 18, 9, 17, 21, 1, 26, 28, 10, 14, 13, 22, 3, 23, 6, 20, 16, 12, 15],
+    [27, 9, 21, 15, 11, 6, 12, 1, 28, 18, 19, 5, 23, 24, 8, 4, 20, 26, 13, 29, 3, 2, 14, 16, 0, 17, 10, 31, 7, 30, 25, 22],
+    [14, 21, 5, 1, 19, 27, 11, 26, 10, 8, 17, 24, 2, 6, 29, 16, 4, 18, 22, 9, 15, 23, 31, 28, 30, 12, 20, 7, 3, 13, 25, 0],
+    [3, 0, 24, 28, 4, 17, 20, 21, 9, 2, 10, 12, 18, 31, 5, 19, 11, 6, 30, 14, 26, 27, 23, 1, 7, 8, 16, 29, 22, 25, 13, 15],
+    [21, 30, 19, 4, 28, 20, 24, 18, 27, 31, 3, 8, 6, 16, 13, 5, 17, 7, 9, 0, 14, 12, 26, 23, 15, 1, 29, 10, 11, 2, 22, 25],
+    [2, 27, 3, 31, 5, 12, 16, 8, 26, 25, 29, 13, 19, 0, 20, 28, 30, 23, 17, 6, 7, 4, 22, 10, 24, 21, 15, 11, 1, 18, 14, 9],
+    [6, 17, 20, 24, 21, 2, 7, 28, 18, 22, 15, 31, 1, 13, 29, 14, 12, 30, 26, 27, 11, 19, 5, 8, 16, 10, 3, 25, 23, 4, 9, 0],
+    [9, 10, 5, 22, 12, 21, 25, 18, 7, 4, 16, 26, 28, 31, 27, 3, 23, 8, 0, 20, 24, 29, 15, 13, 17, 6, 14, 2, 30, 11, 1, 19],
+    [17, 21, 11, 26, 8, 0, 7, 1, 9, 12, 5, 22, 2, 14, 29, 27, 6, 23, 13, 10, 30, 24, 18, 15, 3, 31, 19, 16, 4, 28, 20, 25],
+    [31, 7, 15, 19, 27, 10, 22, 30, 14, 23, 13, 9, 11, 24, 16, 2, 1, 8, 26, 20, 21, 12, 6, 0, 28, 29, 3, 25, 17, 18, 4, 5],
+    [8, 26, 29, 9, 1, 15, 17, 16, 28, 6, 2, 3, 21, 11, 13, 12, 22, 0, 14, 5, 10, 18, 27, 24, 30, 4, 23, 7, 19, 25, 31, 20],
+    [15, 28, 18, 20, 8, 7, 29, 27, 23, 24, 14, 4, 25, 3, 19, 9, 17, 26, 16, 30, 2, 10, 11, 5, 21, 22, 6, 0, 12, 13, 31, 1],
+    [7, 15, 27, 12, 18, 28, 6, 9, 17, 13, 25, 16, 14, 8, 5, 29, 26, 1, 31, 24, 22, 30, 4, 19, 11, 3, 21, 20, 0, 2, 23, 10],
+    [16, 17, 1, 7, 23, 26, 2, 6, 10, 0, 3, 21, 25, 30, 20, 4, 14, 29, 9, 19, 27, 18, 24, 31, 11, 13, 5, 22, 15, 12, 8, 28],
+    [3, 6, 14, 11, 30, 31, 13, 22, 23, 0, 25, 7, 5, 17, 27, 26, 2, 16, 4, 8, 15, 29, 1, 20, 12, 18, 19, 10, 28, 9, 21, 24],
+    [5, 14, 8, 19, 2, 4, 29, 1, 3, 28, 0, 22, 16, 11, 13, 23, 27, 12, 20, 18, 6, 15, 17, 31, 25, 24, 30, 26, 10, 21, 7, 9],
+    [27, 1, 29, 0, 21, 16, 19, 15, 17, 23, 31, 30, 4, 20, 22, 24, 13, 28, 3, 6, 18, 10, 8, 9, 11, 5, 25, 12, 26, 7, 2, 14],
 ]
 
 

time: 115 us -> 113 us (0.983)
  starting transfers between devices: 13 us -> 11.6 us
  waiting for transfers between devices: 11 us -> 9.68 us
    ppermute x1, starting transfers between devices: 11.1 us -> 9.66 us  [shards(): same = lax.ppermute(sent, ROW + COL, pairs)]
    ppermute x1, waiting for transfers between devices: 10.2 us -> 8.86 us  [shards(): same = lax.ppermute(sent, ROW + COL, pairs)]
    all_to_all x1, blocking collectives: 12.9 us -> 14.1 us  [shards(): lax.all_to_all(coded.reshape(nz, slot, rows + 128), 'z', 0, 0, tiled=True)]
where the time goes in v4:
time: 113 us; the launch traced here: 112 us
  blocking collectives  82 us (73%)
  starting transfers between devices  11.6 us (10%)
  waiting for transfers between devices  9.68 us (9%)
  Pallas kernels  7.61 us (7%)
    all_to_all x1, blocking collectives, shards(): coded = lax.all_to_all(coded, 'x', 0, 0, tiled=True)  24.6 us
    all_to_all x1, blocking collectives, shards(): gram = lax.all_to_all(gram, ROW, 0, 0, tiled=True)  23.5 us
    all_to_all x1, blocking collectives, shards(): last = lax.all_to_all(last, COL, 0, 0, tiled=True)  19.9 us
    all_to_all x1, blocking collectives, shards(): lax.all_to_all(coded.reshape(nz, slot, rows + 128), 'z', 0, 0, tiled=True)  14.1 us
    ppermute x1, starting transfers between devices, shards(): same = lax.ppermute(sent, ROW + COL, pairs)  9.66 us
    ppermute x1, waiting for transfers between devices, shards(): same = lax.ppermute(sent, ROW + COL, pairs)  8.86 us
    pallas_call x5, Pallas kernels, run(): pl.pallas_call(kernel, out_shape=shapes, in_specs=[SMEM] * smem + [VMEM]...  5.79 us
  transfers between devices with their start and end apart: 2, of which 2 were waited for; matrix products, arithmetic and copies ran while one was open for 1% of the time, Pallas kernels for 0%

profile of v4, /device:TPU:1, one launch (start us, length us, event | category | flops | bytes accessed | tf_op | source)
XLA Modules:
  0.0 112.3 jit_solution(9004554261796969075)
XLA Ops:
  0.6 0.0 copy-start.4
  0.6 0.0 copy-start.1
  0.7 1.8 %piece.1 = bf16[256,512]{1,0:T(8,128)(2,1)S(1)} custom-call(s32[1]{0:T(128)} %bitcast.1.device_ref, s32[512]{0:T(512)} %constant.26.clone.at_ref, s32[2,8]{1,0:T(2,128)} %mask_ref.4, bf16[2,1024,256]{2,1,0:T(8,128)(2,1)} %factor_ref.3), custom_call_target="tpu_custom_call" | custom-call | tf_op jit(solution)/shard_map/piece/pallas_call | solution.py:310
  2.5 9.7 %collective-permute-start = (bf16[256,512]{1,0:T(8,128)(2,1)S(1)}, bf16[256,512]{1,0:T(8,128)(2,1)S(1)}, u32[]{:S(2)}, u32[]{:S(2)}) collective-permute-start(bf16[256,512]{1,0:T(8,128)(2,1)S(1)} %piece.1), channel_id=1, source_target_pairs={{0,417},{1,129},{2,321},{3,225},{4,161},{5,96},{6,192},{7,1},{8,44... | collective-permute-start | bytes 786440 | tf_op jit(solution)/shard_map/ppermute | solution.py:321
  12.2 8.9 %collective-permute-done.same_ref = bf16[256,512]{1,0:T(8,128)(2,1)S(1)} collective-permute-done((bf16[256,512]{1,0:T(8,128)(2,1)S(1)}, bf16[256,512]{1,0:T(8,128)(2,1)S(1)}, u32[]{:S(2)}, u32[]{:S(2)}) %collective-permute-start) | collective-permute-done | bytes 262176 | tf_op jit(solution)/shard_map/ppermute | solution.py:321
  21.0 1.9 %collective-permute-start.1 = (bf16[256,512]{1,0:T(8,128)(2,1)S(1)}, bf16[256,512]{1,0:T(8,128)(2,1)S(1)}, u32[]{:S(2)}, u32[]{:S(2)}) collective-permute-start(bf16[256,512]{1,0:T(8,128)(2,1)S(1)} %collective-permute-done.same_ref), channel_id=1, source_target_pairs={{0,32},{32,0},{1,33},{33,1},{2,34},{34,2},{3,35},{35,3},{4,36},{36... | collective-permute-start | bytes 786440 | tf_op jit(solution)/shard_map/ppermute | solution.py:322
  22.9 0.0 copy-done.4
  23.0 0.7 copy.12.mask_ref
  23.6 0.8 collective-permute-done.1.other_ref
  24.4 0.0 copy-done.1
  24.4 1.9 %product.1 = s32[4,64,1152]{2,1,0:T(8,128)S(1)} custom-call(s32[8,4]{1,0:T(8,128)} %copy.12.mask_ref, s32[1]{0:T(128)} %bitcast.core_ref, bf16[256,512]{1,0:T(8,128)(2,1)S(1)} %collective-permute-done.same_ref, bf16[256,512]{1,0:T(8,128)(2,1)S(1)} %collective-permute-done.1.other_ref, bf16[1024,512]{1,0:T(8,128)(2,1)S(1)} %copy-done.1), custom_call_target="tpu_custom_call" | custom-call | tf_op jit(solution)/shard_map/product/pallas_call | solution.py:283
  26.3 24.6 %all_to_all.20.in_ref = s32[4,64,1152]{2,1,0:T(8,128)S(1)} all-to-all(s32[4,64,1152]{2,1,0:T(8,128)S(1)} %product.1), channel_id=1, replica_groups=mesh['y'=8,'core'=2,'x'=4,'z'=8] {'x'}, dimensions={0} | all-to-all | bytes 2359296 | tf_op jit(solution)/shard_map/all_to_all | solution.py:331
  50.9 0.0 copy-start
  50.9 0.5 middle.1
  51.3 14.1 %all_to_all.21.in_ref = s32[8,8,1152]{2,1,0:T(8,128)S(1)} all-to-all(s32[8,8,1152]{2,1,0:T(8,128)S(1)} %bitcast.3), channel_id=1, replica_groups=mesh['y'=8,'core'=2,'x'=4,'z'=8] {'z'}, dimensions={0} | all-to-all | bytes 589824 | tf_op jit(solution)/shard_map/all_to_all | solution.py:333
  65.4 0.0 copy-done
  65.4 1.3 %gram.1 = (s32[16,32,128]{2,1,0:T(8,128)S(1)}, s32[32,4,128]{2,1,0:T(4,128)S(1)}, s32[1,128]{1,0:T(1,128)S(1)}) custom-call(s32[2,8]{1,0:T(2,128)} %mask_ref.4, s32[8,8,1152]{2,1,0:T(8,128)S(1)} %all_to_all.21.in_ref, bf16[2,1024,256]{2,1,0:T(8,128)(2,1)S(1)} %copy-done), custom_call_target="tpu_custom_call" | custom-call | tf_op jit(solution)/shard_map/gram/pallas_call | solution.py:283
  66.7 0.0 copy-start.2
  66.7 0.0 copy-start.3
  66.7 23.5 %all_to_all.22.in_ref = s32[16,32,128]{2,1,0:T(8,128)S(1)} all-to-all(s32[16,32,128]{2,1,0:T(8,128)S(1)} %get-tuple-element.8), channel_id=1, replica_groups=mesh['y'=8,'core'=2,'x'=4,'z'=8] {'y','core'}, dimensions={0} | all-to-all | bytes 524288 | tf_op jit(solution)/shard_map/all_to_all | solution.py:340
  90.2 0.3 spread.1
  90.5 19.9 %all_to_all.23.in_ref = s32[32,32,128]{2,1,0:T(8,128)S(1)} all-to-all(s32[32,32,128]{2,1,0:T(8,128)S(1)} %spread.1), channel_id=1, replica_groups=mesh['y'=8,'core'=2,'x'=4,'z'=8] {'x','z'}, dimensions={0} | all-to-all | bytes 1048576 | tf_op jit(solution)/shard_map/all_to_all | solution.py:345
  110.4 0.0 copy-done.2
  110.4 0.0 copy-done.3
  110.4 1.9 %final.1 = (f32[32,256]{1,0:T(8,128)}, f32[256,256]{1,0:T(8,128)}, f32[256,256]{1,0:T(8,128)}, f32[32,256]{1,0:T(8,128)}, f32[256,256]{1,0:T(8,128)}) custom-call(s32[32,32,128]{2,1,0:T(8,128)S(1)} %all_to_all.23.in_ref, bf16[256,256]{1,0:T(8,128)(2,1)S(1)} %copy-done.3, f32[2,256,256]{2,1,0:T(8,128)S(1)} %copy-done.2), custom_call_target="tpu_custom_call" | custom-call | tf_op jit(solution)/shard_map/final/pallas_call | solution.py:283
Async XLA Ops:
  0.6 22.3 %copy-start.4 = (s32[8,4]{0,1:T(4,128)S(1)}, s32[8,4]{0,1:T(4,128)}, u32[]{:S(2)}) copy-start(s32[8,4]{0,1:T(4,128)} %param.8) | copy-start | bytes 388
  0.6 23.8 %copy-start.1 = (bf16[1024,512]{1,0:T(8,128)(2,1)S(1)}, bf16[1024,512]{1,0:T(8,128)(2,1)}, u32[]{:S(2)}) copy-start(bf16[1024,512]{1,0:T(8,128)(2,1)} %inverse_ref.1) | copy-start | bytes 3145732
  2.5 18.5 %collective-permute-start = (bf16[256,512]{1,0:T(8,128)(2,1)S(1)}, bf16[256,512]{1,0:T(8,128)(2,1)S(1)}, u32[]{:S(2)}, u32[]{:S(2)}) collective-permute-start(bf16[256,512]{1,0:T(8,128)(2,1)S(1)} %piece.1), channel_id=1, source_target_pairs={{0,417},{1,129},{2,321},{3,225},{4,161},{5,96},{6,192},{7,1},{8,44... | collective-permute-start | bytes 786440 | tf_op jit(solution)/shard_map/ppermute | solution.py:321
  21.0 3.4 %collective-permute-start.1 = (bf16[256,512]{1,0:T(8,128)(2,1)S(1)}, bf16[256,512]{1,0:T(8,128)(2,1)S(1)}, u32[]{:S(2)}, u32[]{:S(2)}) collective-permute-start(bf16[256,512]{1,0:T(8,128)(2,1)S(1)} %collective-permute-done.same_ref), channel_id=1, source_target_pairs={{0,32},{32,0},{1,33},{33,1},{2,34},{34,2},{3,35},{35,3},{4,36},{36... | collective-permute-start | bytes 786440 | tf_op jit(solution)/shard_map/ppermute | solution.py:322
  50.9 14.5 %copy-start = (bf16[2,1024,256]{2,1,0:T(8,128)(2,1)S(1)}, bf16[2,1024,256]{2,1,0:T(8,128)(2,1)}, u32[]{:S(2)}) copy-start(bf16[2,1024,256]{2,1,0:T(8,128)(2,1)} %factor_ref.3) | copy-start | bytes 3145732
  66.7 43.7 %copy-start.2 = (f32[2,256,256]{2,1,0:T(8,128)S(1)}, f32[2,256,256]{2,1,0:T(8,128)}, u32[]{:S(2)}) copy-start(f32[2,256,256]{2,1,0:T(8,128)} %pivots_ref.1) | copy-start | bytes 1572868
  66.7 43.7 %copy-start.3 = (bf16[256,256]{1,0:T(8,128)(2,1)S(1)}, bf16[256,256]{1,0:T(8,128)(2,1)}, u32[]{:S(2)}) copy-start(bf16[256,256]{1,0:T(8,128)(2,1)} %top_ref.1) | copy-start | bytes 393220

commit v5 on v4

--- a/solution.py
+++ b/solution.py
@@ -48,12 +48,32 @@
     return lax.dot_general(a, b, (((ca,), (cb,)), ((), ())), preferred_element_type=jnp.float32)
 
 
-def encode_rows(high, low):
+def encode_pair(high, low):
     high_step, high_code = scale_of(jnp.max(jnp.abs(high), axis=1, keepdims=True))
     low_step, low_code = scale_of(jnp.max(jnp.abs(low), axis=1, keepdims=True))
-    body = join(whole(high, LIMIT / high_step), whole(low, LIMIT / low_step))
+    return join(whole(high, LIMIT / high_step), whole(low, LIMIT / low_step)), high_code, low_code
+
+
+def encode_rows(high, low):
+    body, high_code, low_code = encode_pair(high, low)
     lane = lax.broadcasted_iota(jnp.int32, (high.shape[0], 128), 1)
     return body, jnp.where(lane < 64, high_code, low_code)
+
+
+def diagonal(count):
+    shape = (count, 128)
+    return lax.broadcasted_iota(jnp.int32, shape, 0), lax.broadcasted_iota(jnp.int32, shape, 1)
+
+
+def decode_tiles(ref, index, count):
+    tiles = ref.shape[1] // count
+    body = [ref[index, j * count : j * count + count, :] for j in range(tiles)]
+    high, low = part(jnp.concatenate(body, axis=1))
+    unit = scale_from(ref[index, tiles * count : tiles * count + 1, :]) * (1.0 / LIMIT)
+    row, lane = diagonal(count)
+    high_unit = jnp.sum(jnp.where(lane == row, unit, 0.0), axis=1, keepdims=True)
+    low_unit = jnp.sum(jnp.where(lane == row + 64, unit, 0.0), axis=1, keepdims=True)
+    return high * high_unit, low * low_unit
 
 
 def decode_rows(ref, index, rows):
@@ -122,21 +142,24 @@
             blocks.append(jnp.concatenate(column, axis=0))
         masked = jnp.concatenate(blocks, axis=1)
         product[:, i * step : i * step + step] = dot(turned[...], masked, 1, 1)
-    count = out_ref.shape[1]
+    count = width // out_ref.shape[0]
     for x in range(out_ref.shape[0]):
-        body, code = encode_rows(
+        body, high_code, low_code = encode_pair(
             product[x * count : x * count + count, :],
             product[width + x * count : width + x * count + count, :],
         )
-        out_ref[x, :, :rows] = body
-        out_ref[x, :, rows:] = code
+        for j in range(rows // 128):
+            out_ref[x, j * count : j * count + count, :] = body[:, j * 128 : j * 128 + 128]
+        row, lane = diagonal(count)
+        codes = jnp.where(lane == row, high_code, 0) + jnp.where(lane == row + 64, low_code, 0)
+        out_ref[x, rows // 128 * count :, :] = jnp.broadcast_to(jnp.sum(codes, axis=0, keepdims=True), (8, 128))
 
 
 def middle_kernel(in_ref, out_ref):
-    rows = in_ref.shape[2] - 128
-    high, low = decode_rows(in_ref, 0, rows)
+    count, rows = out_ref.shape[0], out_ref.shape[1] - 128
+    high, low = decode_tiles(in_ref, 0, count)
     for i in range(1, in_ref.shape[0]):
-        more_high, more_low = decode_rows(in_ref, i, rows)
+        more_high, more_low = decode_tiles(in_ref, i, count)
         high, low = high + more_high, low + more_low
     body, code = encode_rows(high, low)
     out_ref[:, :rows] = body
@@ -323,7 +346,7 @@
 
     coded = call(
         product_kernel,
-        i32(nx, nz * slot, rows + 128),
+        i32(nx, nz * slot * (rows // 128) + 8, 128),
         smem=2,
         scratch=[pltpu.VMEM((2 * width, cols), jnp.bfloat16), pltpu.VMEM((2 * width, rows), jnp.float32)],
         name="product",

time: 113 us -> 111 us (0.982)
  blocking collectives: 82 us -> 80.8 us
    all_to_all x1, blocking collectives: 23.5 us -> 22.2 us  [shards(): gram = lax.all_to_all(gram, ROW, 0, 0, tiled=True)]
where the time goes in v5:
time: 111 us
  blocking collectives  80.8 us (73%)
  starting transfers between devices  11.6 us (10%)
  waiting for transfers between devices  9.68 us (9%)
  Pallas kernels  7.63 us (7%)
    all_to_all x1, blocking collectives, shards(): coded = lax.all_to_all(coded, 'x', 0, 0, tiled=True)  23.6 us
    all_to_all x1, blocking collectives, shards(): gram = lax.all_to_all(gram, ROW, 0, 0, tiled=True)  22.2 us
    all_to_all x1, blocking collectives, shards(): last = lax.all_to_all(last, COL, 0, 0, tiled=True)  19.9 us
    all_to_all x1, blocking collectives, shards(): lax.all_to_all(coded.reshape(nz, slot, rows + 128), 'z', 0, 0, tiled=True)  15 us
    ppermute x1, starting transfers between devices, shards(): same = lax.ppermute(sent, ROW + COL, pairs)  9.66 us
    ppermute x1, waiting for transfers between devices, shards(): same = lax.ppermute(sent, ROW + COL, pairs)  8.86 us
    pallas_call x5, Pallas kernels, run(): pl.pallas_call(kernel, out_shape=shapes, in_specs=[SMEM] * smem + [VMEM]...  5.8 us
  transfers between devices with their start and end apart: 2, of which 2 were waited for; matrix products, arithmetic and copies ran while one was open for 1% of the time, Pallas kernels for 0%

profile of v5, /device:TPU:1, one launch (start us, length us, event | category | flops | bytes accessed | tf_op | source)
XLA Modules:
  0.0 111.1 jit_solution(7416219594890555528)
XLA Ops:
  0.6 0.0 copy-start.4
  0.6 0.0 copy-start.1
  0.7 1.8 %piece.1 = bf16[256,512]{1,0:T(8,128)(2,1)S(1)} custom-call(s32[1]{0:T(128)} %bitcast.1.device_ref, s32[512]{0:T(512)} %constant.26.clone.at_ref, s32[2,8]{1,0:T(2,128)} %mask_ref.4, bf16[2,1024,256]{2,1,0:T(8,128)(2,1)} %factor_ref.3), custom_call_target="tpu_custom_call" | custom-call | tf_op jit(solution)/shard_map/piece/pallas_call | solution.py:333
  2.5 9.7 %collective-permute-start = (bf16[256,512]{1,0:T(8,128)(2,1)S(1)}, bf16[256,512]{1,0:T(8,128)(2,1)S(1)}, u32[]{:S(2)}, u32[]{:S(2)}) collective-permute-start(bf16[256,512]{1,0:T(8,128)(2,1)S(1)} %piece.1), channel_id=1, source_target_pairs={{0,417},{1,129},{2,321},{3,225},{4,161},{5,96},{6,192},{7,1},{8,44... | collective-permute-start | bytes 786440 | tf_op jit(solution)/shard_map/ppermute | solution.py:344
  12.2 8.9 %collective-permute-done.same_ref = bf16[256,512]{1,0:T(8,128)(2,1)S(1)} collective-permute-done((bf16[256,512]{1,0:T(8,128)(2,1)S(1)}, bf16[256,512]{1,0:T(8,128)(2,1)S(1)}, u32[]{:S(2)}, u32[]{:S(2)}) %collective-permute-start) | collective-permute-done | bytes 262176 | tf_op jit(solution)/shard_map/ppermute | solution.py:344
  21.0 1.9 %collective-permute-start.1 = (bf16[256,512]{1,0:T(8,128)(2,1)S(1)}, bf16[256,512]{1,0:T(8,128)(2,1)S(1)}, u32[]{:S(2)}, u32[]{:S(2)}) collective-permute-start(bf16[256,512]{1,0:T(8,128)(2,1)S(1)} %collective-permute-done.same_ref), channel_id=1, source_target_pairs={{0,32},{32,0},{1,33},{33,1},{2,34},{34,2},{3,35},{35,3},{4,36},{36... | collective-permute-start | bytes 786440 | tf_op jit(solution)/shard_map/ppermute | solution.py:345
  22.9 0.0 copy-done.4
  23.0 0.7 copy.12.mask_ref
  23.6 0.8 collective-permute-done.1.other_ref
  24.4 0.0 copy-done.1
  24.4 1.9 %product.1 = s32[4,520,128]{2,1,0:T(8,128)S(1)} custom-call(s32[8,4]{1,0:T(8,128)} %copy.12.mask_ref, s32[1]{0:T(128)} %bitcast.core_ref, bf16[256,512]{1,0:T(8,128)(2,1)S(1)} %collective-permute-done.same_ref, bf16[256,512]{1,0:T(8,128)(2,1)S(1)} %collective-permute-done.1.other_ref, bf16[1024,512]{1,0:T(8,128)(2,1)S(1)} %copy-done.1), custom_call_target="tpu_custom_call" | custom-call | tf_op jit(solution)/shard_map/product/pallas_call | solution.py:306
  26.4 23.6 %all_to_all.20.in_ref = s32[4,520,128]{2,1,0:T(8,128)S(1)} all-to-all(s32[4,520,128]{2,1,0:T(8,128)S(1)} %product.1), channel_id=1, replica_groups=mesh['y'=8,'core'=2,'x'=4,'z'=8] {'x'}, dimensions={0} | all-to-all | bytes 2129920 | tf_op jit(solution)/shard_map/all_to_all | solution.py:354
  50.0 0.0 copy-start
  50.0 0.4 middle.1
  50.4 15.0 %all_to_all.21.in_ref = s32[8,8,1152]{2,1,0:T(8,128)S(1)} all-to-all(s32[8,8,1152]{2,1,0:T(8,128)S(1)} %bitcast.3), channel_id=1, replica_groups=mesh['y'=8,'core'=2,'x'=4,'z'=8] {'z'}, dimensions={0} | all-to-all | bytes 589824 | tf_op jit(solution)/shard_map/all_to_all | solution.py:356
  65.5 0.0 copy-done
  65.5 1.3 %gram.1 = (s32[16,32,128]{2,1,0:T(8,128)S(1)}, s32[32,4,128]{2,1,0:T(4,128)S(1)}, s32[1,128]{1,0:T(1,128)S(1)}) custom-call(s32[2,8]{1,0:T(2,128)} %mask_ref.4, s32[8,8,1152]{2,1,0:T(8,128)S(1)} %all_to_all.21.in_ref, bf16[2,1024,256]{2,1,0:T(8,128)(2,1)S(1)} %copy-done), custom_call_target="tpu_custom_call" | custom-call | tf_op jit(solution)/shard_map/gram/pallas_call | solution.py:306
  66.7 22.2 %all_to_all.22.in_ref = s32[16,32,128]{2,1,0:T(8,128)S(1)} all-to-all(s32[16,32,128]{2,1,0:T(8,128)S(1)} %get-tuple-element.8), channel_id=1, replica_groups=mesh['y'=8,'core'=2,'x'=4,'z'=8] {'y','core'}, dimensions={0} | all-to-all | bytes 524288 | tf_op jit(solution)/shard_map/all_to_all | solution.py:363
  89.0 0.0 copy-start.2
  89.0 0.0 copy-start.3
  89.0 0.3 spread.1
  89.3 19.9 %all_to_all.23.in_ref = s32[32,32,128]{2,1,0:T(8,128)S(1)} all-to-all(s32[32,32,128]{2,1,0:T(8,128)S(1)} %spread.1), channel_id=1, replica_groups=mesh['y'=8,'core'=2,'x'=4,'z'=8] {'x','z'}, dimensions={0} | all-to-all | bytes 1048576 | tf_op jit(solution)/shard_map/all_to_all | solution.py:368
  109.2 0.0 copy-done.2
  109.2 0.0 copy-done.3
  109.2 1.9 %final.1 = (f32[32,256]{1,0:T(8,128)}, f32[256,256]{1,0:T(8,128)}, f32[256,256]{1,0:T(8,128)}, f32[32,256]{1,0:T(8,128)}, f32[256,256]{1,0:T(8,128)}) custom-call(s32[32,32,128]{2,1,0:T(8,128)S(1)} %all_to_all.23.in_ref, bf16[256,256]{1,0:T(8,128)(2,1)S(1)} %copy-done.3, f32[2,256,256]{2,1,0:T(8,128)S(1)} %copy-done.2), custom_call_target="tpu_custom_call" | custom-call | tf_op jit(solution)/shard_map/final/pallas_call | solution.py:306
Async XLA Ops:
  0.6 22.3 %copy-start.4 = (s32[8,4]{0,1:T(4,128)S(1)}, s32[8,4]{0,1:T(4,128)}, u32[]{:S(2)}) copy-start(s32[8,4]{0,1:T(4,128)} %param.8) | copy-start | bytes 388
  0.6 23.8 %copy-start.1 = (bf16[1024,512]{1,0:T(8,128)(2,1)S(1)}, bf16[1024,512]{1,0:T(8,128)(2,1)}, u32[]{:S(2)}) copy-start(bf16[1024,512]{1,0:T(8,128)(2,1)} %inverse_ref.1) | copy-start | bytes 3145732
  2.5 18.5 %collective-permute-start = (bf16[256,512]{1,0:T(8,128)(2,1)S(1)}, bf16[256,512]{1,0:T(8,128)(2,1)S(1)}, u32[]{:S(2)}, u32[]{:S(2)}) collective-permute-start(bf16[256,512]{1,0:T(8,128)(2,1)S(1)} %piece.1), channel_id=1, source_target_pairs={{0,417},{1,129},{2,321},{3,225},{4,161},{5,96},{6,192},{7,1},{8,44... | collective-permute-start | bytes 786440 | tf_op jit(solution)/shard_map/ppermute | solution.py:344
  21.0 3.4 %collective-permute-start.1 = (bf16[256,512]{1,0:T(8,128)(2,1)S(1)}, bf16[256,512]{1,0:T(8,128)(2,1)S(1)}, u32[]{:S(2)}, u32[]{:S(2)}) collective-permute-start(bf16[256,512]{1,0:T(8,128)(2,1)S(1)} %collective-permute-done.same_ref), channel_id=1, source_target_pairs={{0,32},{32,0},{1,33},{33,1},{2,34},{34,2},{3,35},{35,3},{4,36},{36... | collective-permute-start | bytes 786440 | tf_op jit(solution)/shard_map/ppermute | solution.py:345
  50.0 15.5 %copy-start = (bf16[2,1024,256]{2,1,0:T(8,128)(2,1)S(1)}, bf16[2,1024,256]{2,1,0:T(8,128)(2,1)}, u32[]{:S(2)}) copy-start(bf16[2,1024,256]{2,1,0:T(8,128)(2,1)} %factor_ref.3) | copy-start | bytes 3145732
  89.0 20.2 %copy-start.2 = (f32[2,256,256]{2,1,0:T(8,128)S(1)}, f32[2,256,256]{2,1,0:T(8,128)}, u32[]{:S(2)}) copy-start(f32[2,256,256]{2,1,0:T(8,128)} %pivots_ref.1) | copy-start | bytes 1572868
  89.0 20.2 %copy-start.3 = (bf16[256,256]{1,0:T(8,128)(2,1)S(1)}, bf16[256,256]{1,0:T(8,128)(2,1)}, u32[]{:S(2)}) copy-start(bf16[256,256]{1,0:T(8,128)(2,1)} %top_ref.1) | copy-start | bytes 393220
